TPU v7x, 32 devices: a whole 2x2x4 slice. The times are simulated.
32 devices in a mesh: seq: 4 (over z), shard: 4 (over y, core), replica: 2 (over x).
Axes of the slice: x: 2, y: 2, z: 4, core: 2. Of those that a mesh axis runs over, the one named last changes fastest.
Arguments:
- tokens: bfloat16 [8, 2048, 768], P(('shard', 'replica'), 'seq'), may hold values from -6 to 6
- prefix_len: int32 [8], P(('shard', 'replica')), may hold values from 204 to 1024
- w_qkv: bfloat16 [768, 2304], P('shard'), may hold values from -0.3125 to 0.3125
- w_out: bfloat16 [768, 768], P('shard'), may hold values from -1.75 to 1.75
- w_up: bfloat16 [768, 3072], P('shard'), may hold values from -0.21875 to 0.21875
- w_down: bfloat16 [3072, 768], P('shard'), may hold values from -0.109375 to 0.109375
- conv_w: bfloat16 [3, 2304], P(None, 'shard'), may hold values from -3 to 3
- gain_attn: bfloat16 [768], P('shard'), may hold values from 0.25 to 1.75
- gain_ffn: bfloat16 [768], P('shard'), may hold values from 0.25 to 1.75
- cotangent: bfloat16 [8, 2048, 768], P(('shard', 'replica'), 'seq'), may hold values from -6 to 6
Outputs:
- output: bfloat16 [8, 2048, 768], P(('shard', 'replica'), 'seq')
- grad_input: bfloat16 [8, 2048, 768], P(('shard', 'replica'), 'seq')
- grad_qkv: float32 [768, 2304], P('shard')
- grad_out: float32 [768, 768], P('shard')
- grad_up: float32 [768, 3072], P('shard')
- grad_down: float32 [3072, 768], P('shard')
- grad_conv: float32 [3, 2304], P(None, 'shard')
- grad_gain_attn: float32 [768], P('shard')
- grad_gain_ffn: float32 [768], P('shard')
All inputs are finite; a program needn't handle non-finite values.
Results may differ from a plain program's by a relative error of at most 0.019.
Values may be sent and summed in bfloat16 or wider, within the bound.
A program may use at most 192 MiB of HBM per device.

v0:
```python
import functools

import jax
import jax.numpy as jnp
from jax import lax
from jax.experimental import pallas as pl
from jax.experimental.pallas import tpu as pltpu
from jax.sharding import PartitionSpec as P

HEADS = 12
HEAD_DIM=64
NEG=-1e30
F32=jnp.float32
BF=jnp.bfloat16

def nt(a,b):
    return lax.dot_general(a,b,(((1,),(1,)),((),())),preferred_element_type=F32)
def tn(a,b):
    return lax.dot_general(a,b,(((0,),(0,)),((),())),preferred_element_type=F32)

def convolve(proj_ref, conv_ref, wide, parts):
    length = proj_ref.shape[0]
    heads, _, width = wide.shape
    rows = min(512, length)
    for h in range(heads):
        wide[h, 0:8] = jnp.zeros((8, width), F32)
        for c in range(length//rows):
            wide[h, 8+c*rows:8+(c+1)*rows] = proj_ref[c*rows:(c+1)*rows, h*width:(h+1)*width].astype(F32)
    def body(c, _):
        base = pl.multiple_of(c*rows, rows)
        for h in range(heads):
            x = wide[h, pl.ds(base, rows+8)]
            taps = conv_ref[h]
            mixed = taps[0:1]*x[8:] + taps[1:2]*x[7:7+rows] + taps[2:3]*x[6:6+rows]
            for p, ref in enumerate(parts):
                piece = mixed[:, p*HEAD_DIM:(p+1)*HEAD_DIM].astype(BF)
                if p == 0:
                    piece = piece * jnp.asarray(HEAD_DIM**-0.5, BF)
                ref[h, pl.ds(base, rows)] = piece
        return 0
    lax.fori_loop(0, length//rows, body, 0)

def mask_t(i, j, rows, prefix):
    kpos = j*rows + lax.broadcasted_iota(jnp.int32, (rows, 1), 0)
    qpos = i*rows + lax.broadcasted_iota(jnp.int32, (1, rows), 1)
    return (kpos <= qpos) | ((kpos < prefix) & (qpos < prefix))

def mask_n(i, j, rows, prefix):
    qpos = i*rows + lax.broadcasted_iota(jnp.int32, (rows, 1), 0)
    kpos = j*rows + lax.broadcasted_iota(jnp.int32, (1, rows), 1)
    return (kpos <= qpos) | ((kpos < prefix) & (qpos < prefix))

MESH = pl.DeviceIdType.MESH


def remote(src, dst, send, recv, peer):
    return pltpu.make_async_remote_copy(
        src_ref=src, dst_ref=dst, send_sem=send, recv_sem=recv, device_id=peer, device_id_type=MESH
    )


def greet(peers):
    barrier = pltpu.get_barrier_semaphore()
    for peer in peers:
        pl.semaphore_signal(barrier, inc=1, device_id=peer, device_id_type=MESH)
    pl.semaphore_wait(barrier, len(peers))


def split_shard():
    s = lax.axis_index("shard")
    return lax.axis_index("seq"), s // 2, s % 2, lax.axis_index("replica")


class Gather:
    def __init__(self, src, dst, sems, major=False):
        self.src, self.dst, self.major = src, dst, major
        self.sy, self.ry, self.sk, self.rk, self.local = sems
        self.ny = dst.shape[1 if major else 0] // 2
        self.chunks = dst.shape[0 if major else 1]
        self.z, self.y, self.c, self.x = split_shard()
        self.core = (self.z, 2 * self.y + 1 - self.c, self.x)

    def py(self, i):
        return (self.y + i) % self.ny

    def dy(self, i):
        return (self.z, 2 * self.py(i) + self.c, self.x)

    def peers(self):
        return [self.core] + [self.dy(i) for i in range(1, self.ny)]

    def slot(self, p, core, j):
        shard = 2 * p + core
        return self.dst.at[j, shard] if self.major else self.dst.at[shard, j]

    def own(self):
        shard = 2 * self.y + self.c
        dst = self.dst.at[:, shard] if self.major else self.dst.at[shard]
        return pltpu.make_async_copy(self.src, dst, self.local.at[0])

    def over_y(self, j, i):
        slot = self.slot(self.y, self.c, j)
        return remote(self.src.at[j], slot, self.sy.at[j, self.py(i)], self.ry.at[j, self.y], self.dy(i))

    def to_core(self, j):
        slot = self.slot(self.y, self.c, j)
        return remote(self.src.at[j], slot, self.sk.at[j, self.y], self.rk.at[j, self.y], self.core)

    def pass_on(self, j, i):
        ref = self.slot(self.py(i), self.c, j)
        return remote(ref, ref, self.sk.at[j, self.py(i)], self.rk.at[j, self.py(i)], self.core)

    def send(self, j):
        for i in range(1, self.ny):
            self.over_y(j, i).start()
        self.to_core(j).start()

    def start(self):
        for j in range(self.chunks):
            self.send(j)
        self.own().start()

    def relay(self, j):
        for i in range(1, self.ny):
            ref = self.slot(self.py(i), self.c, j)
            remote(ref, ref, self.sy.at[j, self.py(i)], self.ry.at[j, self.py(i)], self.dy(i)).wait_recv()
            self.pass_on(j, i).start()

    def arrive(self, j):
        for i in range(self.ny):
            ref = self.slot(self.py(i), 1 - self.c, j)
            remote(ref, ref, self.sk.at[j, self.py(i)], self.rk.at[j, self.py(i)], self.core).wait_recv()

    def sent(self, j):
        self.to_core(j).wait_send()
        for i in range(1, self.ny):
            self.over_y(j, i).wait_send()
            self.pass_on(j, i).wait_send()

    def finish(self):
        self.own().wait()
        for j in range(self.chunks):
            self.arrive(j)
            self.sent(j)

    @staticmethod
    def sems(shards, chunks):
        return [pltpu.SemaphoreType.DMA((chunks, shards // 2))] * 4 + [pltpu.SemaphoreType.DMA((1,))]


def gather_kernel(
    tok_ref, small_ref, qkv_ref, out_ref, up_ref,
    normed_ref, proj_ref, small_all, qkv_all, out_all, up_all,
    toks, sl, sr, rl, rr, *sems,
):
    blocks, rows, width = toks.shape
    _, shards, depth, columns = qkv_all.shape
    small, qkv, out, up = (
        Gather(src, dst, sems[5 * i : 5 * i + 5], major=i == 1)
        for i, (src, dst) in enumerate(
            ((small_ref, small_all), (qkv_ref, qkv_all), (out_ref, out_all), (up_ref, up_all))
        )
    )
    z, y, c, x = split_shard()
    shard = 2 * y + c
    left, right = (z - 1, shard, x), (z + 1, shard, x)
    has_left, has_right = z > 0, z < blocks - 1
    greet(small.peers() + [((z + i) % blocks, shard, x) for i in range(1, blocks)])

    def go_left(b, src):
        return remote(src, toks.at[b], sl.at[b], rr.at[b], left)

    def go_right(b, src):
        return remote(src, toks.at[b], sr.at[b], rl.at[b], right)

    small.start()
    qkv.send(z)
    qkv.own().start()

    @pl.when(has_left)
    def _():
        go_left(z, tok_ref).start()

    @pl.when(has_right)
    def _():
        go_right(z, tok_ref).start()

    out.start()
    up.start()
    for i in range(1, blocks):
        qkv.send((z + i) % blocks)
    small.relay(0)
    qkv.relay(z)
    small.finish()
    qkv.own().wait()
    qkv.arrive(z)
    gain = jnp.concatenate([small_all[s, 0, 0:1, :depth] for s in range(shards)], axis=1).astype(F32)
    weight = qkv_all[z].reshape(shards * depth, columns)

    def project(b, values):
        at = pl.ds(pl.multiple_of(b * rows, rows), rows)
        values = values.astype(F32)
        scale = lax.rsqrt(jnp.mean(values * values, axis=-1, keepdims=True) + 1e-06)
        normed = values * scale * gain
        proj_ref[at] = jnp.dot(normed.astype(BF), weight, preferred_element_type=F32).astype(BF)
        normed_ref[:, at] = jnp.transpose(normed).astype(BF)

    project(z, tok_ref[...])
    for d in range(1, blocks):
        before, after = z - d, z + d

        @pl.when(before >= 0)
        def _():
            go_right(before, toks.at[before]).wait_recv()

            @pl.when(has_right)
            def _():
                go_right(before, toks.at[before]).start()

        @pl.when(after < blocks)
        def _():
            go_left(after, toks.at[after]).wait_recv()

            @pl.when(has_left)
            def _():
                go_left(after, toks.at[after]).start()

        @pl.when(before >= 0)
        def _():
            project(before, toks[before])

        @pl.when(after < blocks)
        def _():
            project(after, toks[after])

        if d == 1:
            out.relay(0)
        last = up.chunks * d // (blocks - 1)
        for j in range(up.chunks * (d - 1) // (blocks - 1), last):
            up.relay(j)

    for i in range(1, blocks):
        qkv.relay((z + i) % blocks)
    out.finish()
    up.finish()
    for i in range(1, blocks):
        qkv.arrive((z + i) % blocks)
    for j in range(blocks):
        qkv.sent(j)

    def sent(b, _):
        @pl.when((b <= z) & has_right)
        def _():
            go_right(b, toks.at[b]).wait_send()

        @pl.when((b >= z) & has_left)
        def _():
            go_left(b, toks.at[b]).wait_send()

        return 0

    lax.fori_loop(0, blocks, sent, 0)


def gather_all(tokens, small, qkv, out, up, blocks, shards):
    rows, width = tokens.shape
    vm = pl.BlockSpec(memory_space=pltpu.VMEM)
    hbm = pl.BlockSpec(memory_space=pl.ANY)
    cut = 4
    arrays = [
        small[None],
        qkv,
        out[None],
        up.reshape(cut, up.shape[0] // cut, up.shape[1]),
    ]
    dma = pltpu.SemaphoreType.DMA
    sems = [dma((blocks,))] * 4
    for array in arrays:
        sems += Gather.sems(shards, array.shape[0])
    return pl.pallas_call(
        gather_kernel,
        out_shape=[
            jax.ShapeDtypeStruct((width, blocks * rows), BF),
            jax.ShapeDtypeStruct((blocks * rows, qkv.shape[2]), BF),
        ]
        + [
            jax.ShapeDtypeStruct(
                (blocks, shards) + array.shape[1:] if i == 1 else (shards,) + array.shape, BF
            )
            for i, array in enumerate(arrays)
        ],
        in_specs=[vm] * 5,
        out_specs=[vm] * 4 + [hbm] * 2,
        scratch_shapes=[pltpu.VMEM((blocks, rows, width), BF)] + sems,
        compiler_params=pltpu.CompilerParams(
            vmem_limit_bytes=60 * 1024 * 1024, collective_id=4, has_side_effects=True
        ),
        name="gather_all",
    )(tokens, *arrays)


def fwd_kernel(prefix_ref, proj_ref, conv_ref, down_ref, own_ref, lse_ref, rows_ref, down_all, wide, qs, ks, vs, m_s, l_s, acc_s, o_s, r_s, send, recv, *sems):
    heads = qs.shape[0]
    length = proj_ref.shape[0]
    blocks = own_ref.shape[1]
    rows = length // blocks
    prefix = prefix_ref[0]
    z, s_at, x = lax.axis_index("seq"), lax.axis_index("shard"), lax.axis_index("replica")

    def block_copy(h, i, at):
        return remote(o_s.at[h, i], r_s.at[at * heads + h], send.at[h, i], recv.at[h, at], (i, s_at, x))

    down = Gather(down_ref, down_all, sems)
    greet([((z + i) % blocks, s_at, x) for i in range(1, blocks)] + down.peers())
    down.start()
    convolve(proj_ref, conv_ref, wide, (qs, ks, vs))
    def head(h, _):
        for j in range(down.chunks):
            @pl.when(h == 1 + (j + 1) // 2)
            def _():
                down.relay(j)
        def qblock(i, _):
            q = qs[h, pl.ds(pl.multiple_of(i*rows, rows), rows)]
            m_s[...] = jnp.full((1, rows), NEG, F32)
            l_s[...] = jnp.zeros((1, rows), F32)
            acc_s[...] = jnp.zeros((HEAD_DIM, rows), F32)
            def step(j, masked):
                at = pl.ds(pl.multiple_of(j*rows, rows), rows)
                s = nt(ks[h, at], q)
                if masked:
                    s = jnp.where(mask_t(i, j, rows, prefix), s, NEG)
                m_old = m_s[...]
                m_new = jnp.maximum(m_old, jnp.max(s, axis=0, keepdims=True))
                p = jnp.exp(s - m_new)
                a = jnp.exp(m_old - m_new)
                m_s[...] = m_new
                l_s[...] = a*l_s[...] + jnp.sum(p, axis=0, keepdims=True)
                acc_s[...] = a*acc_s[...] + tn(vs[h, at], p.astype(BF))
                return 0
            lax.fori_loop(0, i, lambda j, _: step(j, False), 0)
            lax.fori_loop(i, jnp.maximum(i+1, blocks//2), lambda j, _: step(j, True), 0)
            l = l_s[...]
            done = (acc_s[...]/l).astype(BF)
            o_s[h, i] = done
            own_ref[h, i] = done
            @pl.when(i != z)
            def _():
                block_copy(h, i, z).start()
            lse = m_s[...] + jnp.log(l)
            lse_ref[h, :, pl.ds(pl.multiple_of(i*rows, rows), rows)] = jnp.broadcast_to(lse, (8, rows))
            return 0
        lax.fori_loop(0, blocks, qblock, 0)
        r_s[z * heads + h] = o_s[h, z]
        return 0
    lax.fori_loop(0, heads, head, 0)
    for j in range(down.chunks):
        if 1 + (j + 1) // 2 >= heads:
            down.relay(j)
    down.finish()
    def finish(h, _):
        for i in range(1, blocks):
            there = (z + i) % blocks
            block_copy(h, there, there).wait_recv()
            block_copy(h, there, z).wait_send()
        return 0
    lax.fori_loop(0, heads, finish, 0)
    rows_ref[...] = r_s[...]

def attention_fwd(prefix, proj, conv, down, blocks, shards):
    length, width = proj.shape
    heads = width//(3*HEAD_DIM)
    rows = length // blocks
    vm = pl.BlockSpec(memory_space=pltpu.VMEM)
    own = (heads, blocks, HEAD_DIM, rows)
    every = (heads * blocks, HEAD_DIM, rows)
    return pl.pallas_call(
        fwd_kernel,
        out_shape=(jax.ShapeDtypeStruct(own, BF), jax.ShapeDtypeStruct((heads, 8, length), F32), jax.ShapeDtypeStruct(every, BF),
            jax.ShapeDtypeStruct((shards,) + down.shape, BF)),
        in_specs=[pl.BlockSpec(memory_space=pltpu.SMEM), vm, vm, vm],
        out_specs=(vm, vm, vm, pl.BlockSpec(memory_space=pl.ANY)),
        scratch_shapes=[pltpu.VMEM((heads, 8+length, 3*HEAD_DIM), F32)] + [pltpu.VMEM((heads, length, HEAD_DIM), BF)]*3 + [
            pltpu.VMEM((1,rows),F32), pltpu.VMEM((1,rows),F32), pltpu.VMEM((HEAD_DIM,rows),F32), pltpu.VMEM(own,BF), pltpu.VMEM(every,BF),
            pltpu.SemaphoreType.DMA((heads, blocks)), pltpu.SemaphoreType.DMA((heads, blocks))] + Gather.sems(shards, down.shape[0]),
        compiler_params=pltpu.CompilerParams(vmem_limit_bytes=60*1024*1024, collective_id=2, has_side_effects=True),
        cost_estimate=pl.CostEstimate(flops=4*heads*length*length*HEAD_DIM, bytes_accessed=length*width*2, transcendentals=heads*length*length),
        name="attention_fwd",
    )(prefix, proj, conv, down)

class Sums:
    def __init__(self, parts, out_ref, bufs, sems, nz):
        self.parts, self.out = parts, out_ref
        self.a, self.b, self.c, self.near, self.far = bufs
        self.sa, self.ra, self.sb, self.rb, self.sc, self.rc, self.sz, self.rz, self.sf, self.rf = sems
        self.chunks, self.ny = self.a.shape[:2]
        self.nx = self.c.shape[1]
        self.nz = nz
        self.half = self.c.shape[2]
        self.piece = self.half // nz
        self.me = split_shard()
        z, y, c, x = self.me
        self.core = (z, 2 * y + 1 - c, x)
        self.low, self.high = z % 2, z // 2
        self.one = (z + 1 - 2 * self.low, 2 * y + c, x)
        self.two = (z + 2 - 4 * self.high, 2 * y + c, x)

    def py(self, i):
        return (self.me[1] + i) % self.ny

    def px(self, i):
        return (self.me[3] + i) % self.nx

    def pz(self, i):
        return (self.me[0] + i) % self.nz

    def dy(self, i):
        z, y, c, x = self.me
        return (z, 2 * self.py(i) + c, x)

    def dx(self, i):
        z, y, c, x = self.me
        return (z, 2 * y + c, self.px(i))

    def dz(self, i):
        z, y, c, x = self.me
        return (self.pz(i), 2 * y + c, x)

    def peers(self):
        out = [self.core] + [self.dy(i) for i in range(1, self.ny)]
        out += [self.dx(i) for i in range(1, self.nx)]
        return out + [self.dz(i) for i in range(1, self.nz)]

    def copy_a(self, k, src):
        return remote(src, self.a.at[k], self.sa.at[k], self.ra.at[k], self.core)

    def start(self):
        c = self.me[2]
        for ref, first, count in self.parts:
            for j in range(count):
                src = ref.at[:, 1 - c, j]
                self.copy_a(first + j, src).start()

    def copy_b(self, k, i, there):
        slot = self.ny - i - 1 if there else i - 1
        return remote(self.a.at[k, self.py(i)], self.b.at[k, slot], self.sb.at[k, i - 1], self.rb.at[k, slot], self.dy(i))

    def stage_b(self, k):
        c = self.me[2]
        self.copy_a(k, self.a.at[k]).wait_recv()
        for i in list(range(1, self.ny)) + [0]:
            p = self.py(i)
            for ref, first, count in self.parts:
                @pl.when((k >= first) & (k < first + count))
                def _():
                    j = jnp.clip(k - first, 0, count - 1)
                    self.a[k, p] = (self.a[k, p].astype(F32) + ref[p, c, j].astype(F32)).astype(BF)
            if i:
                self.copy_b(k, i, True).start()

    def copy_c(self, k, i, there):
        slot = self.me[3] if there else self.px(i)
        src = self.a.at[k, self.me[1], pl.ds(self.px(i) * self.half, self.half)]
        return remote(src, self.c.at[k, slot], self.sc.at[k, self.px(i)], self.rc.at[k, slot], self.dx(i))

    def stage_c(self, k):
        y = self.me[1]
        total = self.a[k, y].astype(F32)
        for i in range(1, self.ny):
            self.copy_b(k, i, False).wait_recv()
            total = total + self.b[k, i - 1].astype(F32)
        for i in range(1, self.ny):
            self.copy_b(k, i, True).wait_send()
        self.a[k, y] = total.astype(BF)
        for i in range(1, self.nx):
            self.copy_c(k, i, True).start()

    def pieces(self, low, high, count):
        return pl.ds(self.me[3] * self.half + (2 * low + high) * self.piece, count * self.piece)

    def copy_z(self, k, stage):
        if stage == 0:
            src, dst, peer = self.a.at[k, self.me[1], self.pieces(1 - self.low, 0, 2)], self.near.at[k], self.one
        elif stage == 1:
            src, dst, peer = self.a.at[k, self.me[1], self.pieces(self.low, 1 - self.high, 1)], self.far.at[k], self.two
        elif stage == 2:
            src = dst = self.out.at[k, self.pieces(self.low, self.high, 1)]
            peer = self.two
        else:
            src = dst = self.out.at[k, self.pieces(self.low, 0, 2)]
            peer = self.one
        return remote(src, dst, self.sz.at[k, stage], self.rz.at[k, stage], peer)

    def stage_d(self, k):
        z, y, c, x = self.me
        mine = pl.ds(x * self.half, self.half)
        total = self.a[k, y, mine].astype(F32)
        for i in range(1, self.nx):
            self.copy_c(k, i, False).wait_recv()
            total = total + self.c[k, self.px(i)].astype(F32)
        for i in range(1, self.nx):
            self.copy_c(k, i, True).wait_send()
        self.a[k, y, mine] = total.astype(BF)
        self.copy_z(k, 0).start()

    def stage_near(self, k):
        y = self.me[1]
        self.copy_z(k, 0).wait_recv()
        self.copy_z(k, 0).wait_send()
        mine = self.pieces(self.low, 0, 2)
        self.a[k, y, mine] = (self.a[k, y, mine].astype(F32) + self.near[k].astype(F32)).astype(BF)
        self.copy_z(k, 1).start()

    def stage_far(self, k):
        self.copy_z(k, 1).wait_recv()
        mine = self.pieces(self.low, self.high, 1)
        self.out[k, mine] = (self.a[k, self.me[1], mine].astype(F32) + self.far[k].astype(F32)).astype(BF)
        self.copy_z(k, 2).start()

    def stage_back(self, k):
        ref = self.out.at[k, self.pieces(self.low, 1 - self.high, 1)]
        remote(ref, ref, self.sz.at[k, 2], self.rz.at[k, 2], self.two).wait_recv()
        self.copy_z(k, 3).start()

    def copy_f(self, k, i, there):
        slot = self.me[3] if there else self.px(i)
        ref = self.out.at[k, pl.ds(slot * self.half, self.half)]
        return remote(ref, ref, self.sf.at[k, self.px(i)], self.rf.at[k, slot], self.dx(i))

    def stage_f(self, k):
        ref = self.out.at[k, self.pieces(1 - self.low, 0, 2)]
        remote(ref, ref, self.sz.at[k, 3], self.rz.at[k, 3], self.one).wait_recv()
        for i in range(1, self.nx):
            self.copy_f(k, i, True).start()

    def step(self, t):
        for lag, stage in enumerate(
            (self.stage_c, self.stage_d, self.stage_near, self.stage_far, self.stage_back, self.stage_f)
        ):
            @pl.when((t >= lag) & (t < self.chunks + lag))
            def _():
                stage(t - lag)

    def finish(self):
        def body(k, _):
            for i in range(1, self.nx):
                self.copy_f(k, i, False).wait_recv()
            self.copy_a(k, self.a.at[k]).wait_send()
            for i in range(1, self.nx):
                self.copy_f(k, i, True).wait_send()
            for stage in range(1, 4):
                self.copy_z(k, stage).wait_send()
            return 0

        lax.fori_loop(0, self.chunks, body, 0)

    @staticmethod
    def sems(chunks, ny, nx):
        out = [pltpu.SemaphoreType.DMA((chunks,))] * 2
        for n in (ny - 1, nx, 4, nx):
            out += [pltpu.SemaphoreType.DMA((chunks, n))] * 2
        return out


class OwnSums:
    def __init__(self, sums, part, out, bufs, sems):
        self.s, self.part, self.out = sums, part, out
        self.a, self.b, self.c = bufs
        self.sa, self.ra, self.sb, self.rb, self.sc, self.rc, self.se, self.re, self.sf, self.rf = sems
        self.half = self.c.shape[2]

    def copy_a(self, h):
        return remote(self.part.at[h, :, 1 - self.s.me[2]], self.a.at[h], self.sa.at[h], self.ra.at[h], self.s.core)

    def copy_b(self, h, i, there):
        s = self.s
        slot = s.ny - i - 1 if there else i - 1
        return remote(self.a.at[h, s.py(i)], self.b.at[h, slot], self.sb.at[h, i - 1], self.rb.at[h, slot], s.dy(i))

    def copy_c(self, h, i, there):
        s = self.s
        slot = s.me[3] if there else s.px(i)
        src = self.a.at[h, s.me[1], pl.ds(s.px(i) * self.half, self.half)]
        return remote(src, self.c.at[h, slot], self.sc.at[h, s.px(i)], self.rc.at[h, slot], s.dx(i))

    def copy_e(self, h, i, there):
        s = self.s
        slot = s.me[0] if there else s.pz(i)
        ref = self.out.at[h, slot, pl.ds(s.me[3] * self.half, self.half)]
        return remote(ref, ref, self.se.at[h, s.pz(i)], self.re.at[h, slot], s.dz(i))

    def copy_f(self, h, i, there):
        s = self.s
        slot = s.me[3] if there else s.px(i)
        ref = self.out.at[h, :, pl.ds(slot * self.half, self.half)]
        return remote(ref, ref, self.sf.at[h, s.px(i)], self.rf.at[h, slot], s.dx(i))

    def stage_b(self, h):
        s = self.s
        self.copy_a(h).wait_recv()
        for i in list(range(1, s.ny)) + [0]:
            p = s.py(i)
            self.a[h, p] = (self.a[h, p].astype(F32) + self.part[h, p, s.me[2]].astype(F32)).astype(BF)
            if i:
                self.copy_b(h, i, True).start()

    def stage_c(self, h):
        s = self.s
        total = self.a[h, s.me[1]].astype(F32)
        for i in range(1, s.ny):
            self.copy_b(h, i, False).wait_recv()
            total = total + self.b[h, i - 1].astype(F32)
        self.a[h, s.me[1]] = total.astype(BF)
        for i in range(1, s.nx):
            self.copy_c(h, i, True).start()

    def stage_e(self, h):
        s = self.s
        mine = pl.ds(s.me[3] * self.half, self.half)
        total = self.a[h, s.me[1], mine].astype(F32)
        for i in range(1, s.nx):
            self.copy_c(h, i, False).wait_recv()
            total = total + self.c[h, s.px(i)].astype(F32)
        self.out[h, s.me[0], mine] = total.astype(BF)
        for i in range(1, s.nz):
            self.copy_e(h, i, True).start()

    def stage_f(self, h):
        s = self.s
        for i in range(1, s.nz):
            self.copy_e(h, i, False).wait_recv()
        for i in range(1, s.nx):
            self.copy_f(h, i, True).start()

    def stages(self):
        return (self.stage_b, self.stage_c, self.stage_e, self.stage_f)

    def finish(self, h):
        s = self.s
        self.copy_a(h).wait_send()
        for i in range(1, s.ny):
            self.copy_b(h, i, True).wait_send()
        for i in range(1, s.nx):
            self.copy_c(h, i, True).wait_send()
            self.copy_f(h, i, False).wait_recv()
            self.copy_f(h, i, True).wait_send()
        for i in range(1, s.nz):
            self.copy_e(h, i, True).wait_send()

    @staticmethod
    def sems(heads, ny, nx, nz):
        out = [pltpu.SemaphoreType.DMA((heads,))] * 2
        for n in (ny - 1, nx, nz, nx):
            out += [pltpu.SemaphoreType.DMA((heads, n))] * 2
        return out


def bwd_kernel(counts, *refs):
    refs = list(refs)

    def take(n):
        out = refs[:n]
        del refs[:n]
        return out

    prefix_ref, proj_ref, conv_ref, do_ref, o_ref, lse_ref, normed_ref = take(7)
    part_refs = take(len(counts))
    gp_ref, sum_ref, own_ref = take(3)
    wide, qs, ks, vs, dos, delta, dq, dk, dv, gk, gv, gwide, gp_s, gpt, own_part = take(15)
    send, recv, gsend, grecv = take(4)
    bufs = take(5)
    sems = take(10)
    own_bufs = take(3)
    own_sems = take(10)
    heads, length, _ = qs.shape
    width = gwide.shape[1]
    blocks = dos.shape[1]
    rows = length//blocks
    prefix = prefix_ref[0]
    parts = []
    first = 0
    for ref, count in zip(part_refs, counts):
        parts.append((ref, first, count))
        first += count
    sums = Sums(parts, sum_ref, bufs, sems, blocks)
    own = OwnSums(sums, own_part, own_ref, own_bufs, own_sems)
    z, y, c, x = sums.me
    greet(sums.peers())
    sums.start()

    def block_copy(h, i, at):
        return remote(do_ref.at[i * heads + h], dos.at[h, at], send.at[h, i], recv.at[h, at], (i, 2 * y + c, x))

    for h in range(heads):
        for i in range(1, blocks):
            block_copy(h, (z + i) % blocks, z).start()
        dos[h, z] = do_ref[z * heads + h]

    def gp_copy(h, i, at):
        return remote(gpt.at[h, i], gp_ref.at[at * heads + h], gsend.at[h, i], grecv.at[h, at], (i, 2 * y + c, x))

    convolve(proj_ref, conv_ref, wide, (qs, ks, vs))

    def head(h, _):
        for i in range(1, blocks):
            there = (z + i) % blocks
            block_copy(h, there, there).wait_recv()
        for i in range(blocks):
            prod = dos[h, i].astype(F32) * o_ref[h, i].astype(F32)
            delta[i] = jnp.broadcast_to(jnp.sum(prod, axis=0, keepdims=True), (8, rows))
        dq[...] = jnp.zeros(dq.shape, F32)
        def kblock(j, _):
            t = h*blocks + j
            @pl.when(t < sums.chunks)
            def _():
                sums.stage_b(t)
            turn = (2*t)//3
            @pl.when((turn > 0) & ((2*t)%3 != 2))
            def _():
                sums.step(turn - 1)
            for n, stage in enumerate(own.stages()):
                @pl.when((h > 0) & (j == n))
                def _():
                    stage(h - 1)
            kat = pl.ds(pl.multiple_of(j*rows, rows), rows)
            k = ks[h, kat]; v = vs[h, kat]
            dk[...] = jnp.zeros(dk.shape, F32)
            dv[...] = jnp.zeros(dv.shape, F32)
            def step(i, masked):
                qat = pl.ds(pl.multiple_of(i*rows, rows), rows)
                q = qs[h, qat]; do = dos[h, i]
                s = nt(k, q)
                p = jnp.exp(s - lse_ref[h, 0:1, qat])
                if masked:
                    p = jnp.where(mask_t(i, j, rows, prefix), p, 0.0)
                dv[...] += nt(p.astype(BF), do)
                dp = jnp.dot(v, do, preferred_element_type=F32)
                ds = (p*(dp - delta[i, 0:1])).astype(BF)
                dk[...] += jnp.dot(ds, q, preferred_element_type=F32)
                dq[qat] += tn(ds, k)
                return 0
            lax.fori_loop(j+1, blocks, lambda i, _: step(i, False), 0)
            lax.fori_loop(jnp.where(j < blocks//2, 0, j), j+1, lambda i, _: step(i, True), 0)
            gk[kat] = dk[...].astype(BF)
            gv[kat] = dv[...].astype(BF)
            return 0
        lax.fori_loop(0, blocks, kblock, 0)
        def fill(c, _):
            at = pl.ds(pl.multiple_of(c*rows, rows), rows)
            gq = (dq[at]*(HEAD_DIM**-0.5)).astype(BF)
            gwide[at] = jnp.concatenate([gq, gk[at], gv[at]], axis=1).astype(F32)
            return 0
        lax.fori_loop(0, blocks, fill, 0)
        taps = conv_ref[h]
        def out(i, total):
            base = pl.multiple_of(i*rows, rows)
            g = gwide[pl.ds(base, rows+8)]
            w = wide[h, pl.ds(base, rows+8)]
            g0 = g[:rows]
            gp = taps[0:1]*g0 + taps[1:2]*g[1:rows+1] + taps[2:3]*g[2:rows+2]
            gp_s[pl.ds(base, rows)] = gp.astype(BF)
            gpt[h, i] = jnp.transpose(gp).astype(BF)
            @pl.when(i != z)
            def _():
                gp_copy(h, i, z).start()
            add = [jnp.sum(g0*w[8-t:8-t+rows], axis=0, keepdims=True) for t in range(3)]
            return tuple(a+b for a, b in zip(total, add))
        total = lax.fori_loop(0, blocks, out, tuple(jnp.zeros((1, width), F32) for _ in range(3)))
        gp_ref[z * heads + h] = gpt[h, z]
        grad = jnp.dot(normed_ref[...], gp_s[...], preferred_element_type=F32).astype(BF)
        shape = own_part.shape[1:]
        mine = grad.shape[0] // (8 * shape[0] * shape[1])
        own_part[h, :, :, 0:mine] = grad.reshape(shape[0], shape[1], mine, 8, width)
        extra = jnp.concatenate(list(total) + [jnp.zeros((5, width), F32)], axis=0).astype(BF)
        own_part[h, :, :, mine] = jnp.broadcast_to(extra, shape[:2] + (8, width))
        for spare in range(mine + 1, shape[2]):
            own_part[h, :, :, spare] = jnp.zeros(shape[:2] + (8, width), BF)
        own.copy_a(h).start()
        return 0
    gwide[length:length+8] = jnp.zeros((8, width), F32)
    lax.fori_loop(0, heads, head, 0)
    steps = heads*blocks
    turns = (2*(steps - 1))//3
    def rest(t, _):
        sums.stage_b(t)
        return 0
    lax.fori_loop(steps, sums.chunks, rest, 0)
    for n, stage in enumerate(own.stages()):
        sums.step(turns + n)
        stage(heads - 1)
    count = len(own.stages())
    def tail(t, _):
        sums.step(t)
        return 0
    lax.fori_loop(turns + count, max(sums.chunks + 5, turns + count), tail, 0)
    sums.finish()
    def done(h, _):
        own.finish(h)
        for i in range(1, blocks):
            there = (z + i) % blocks
            block_copy(h, there, z).wait_send()
            gp_copy(h, there, there).wait_recv()
            gp_copy(h, there, z).wait_send()
        return 0
    lax.fori_loop(0, heads, done, 0)

def attention_bwd(prefix, proj, conv, do, o, lse, normed, parts, shape):
    length = proj.shape[0]
    heads, blocks = o.shape[:2]
    width = 3 * HEAD_DIM
    rows = length // blocks
    counts = tuple(part.shape[2] for part in parts)
    ny, _, _, units = parts[0].shape[:4]
    unit = parts[0].shape[4:]
    nx = shape["replica"]
    chunks = sum(counts)
    half = units // nx
    own_units = -(-(normed.shape[0] // (16 * ny) + 1) // nx) * nx
    own_unit = (8, width)
    vm = pl.BlockSpec(memory_space=pltpu.VMEM)
    dma = pltpu.SemaphoreType.DMA
    per = pltpu.VMEM((heads, length, HEAD_DIM), BF)
    return pl.pallas_call(
        functools.partial(bwd_kernel, counts),
        out_shape=(
            jax.ShapeDtypeStruct((heads * blocks, width, rows), BF),
            jax.ShapeDtypeStruct((chunks, units) + unit, BF),
            jax.ShapeDtypeStruct((heads, blocks, own_units) + own_unit, BF),
        ),
        in_specs=[pl.BlockSpec(memory_space=pltpu.SMEM)] + [vm]*(6 + len(parts)),
        out_specs=(vm, vm, vm),
        scratch_shapes=[pltpu.VMEM((heads, 8+length, width), F32), per, per, per, pltpu.VMEM(o.shape, BF), pltpu.VMEM((blocks, 8, rows), F32),
            pltpu.VMEM((length, HEAD_DIM), F32), pltpu.VMEM((rows, HEAD_DIM), F32), pltpu.VMEM((rows, HEAD_DIM), F32),
            pltpu.VMEM((length, HEAD_DIM), BF), pltpu.VMEM((length, HEAD_DIM), BF),
            pltpu.VMEM((length+8, width), F32), pltpu.VMEM((length, width), BF), pltpu.VMEM((heads, blocks, width, rows), BF),
            pltpu.VMEM((heads, ny, 2, own_units) + own_unit, BF)]
            + [dma((heads, blocks))] * 4
            + [pltpu.VMEM((chunks, ny, units) + unit, BF), pltpu.VMEM((chunks, ny - 1, units) + unit, BF),
            pltpu.VMEM((chunks, nx, half) + unit, BF), pltpu.VMEM((chunks, half // 2) + unit, BF), pltpu.VMEM((chunks, half // 4) + unit, BF)]
            + Sums.sems(chunks, ny, nx)
            + [pltpu.VMEM((heads, ny, own_units) + own_unit, BF), pltpu.VMEM((heads, ny - 1, own_units) + own_unit, BF),
            pltpu.VMEM((heads, nx, own_units // nx) + own_unit, BF)]
            + OwnSums.sems(heads, ny, nx, blocks),
        compiler_params=pltpu.CompilerParams(vmem_limit_bytes=67043328, collective_id=3, has_side_effects=True),
        cost_estimate=pl.CostEstimate(flops=10*heads*length*length*HEAD_DIM, bytes_accessed=length*width*4, transcendentals=heads*length*length),
        name="attention_bwd",
    )(prefix, proj, conv, do, o, lse, normed, *parts)


def rms_scale(values):
    return lax.rsqrt(jnp.mean(values * values, axis=-1, keepdims=True) + 1e-06)


def norm_back(values, scale_rows, gain, upstream):
    weighted = upstream * gain
    grad_values = scale_rows * weighted - values * scale_rows**3 * jnp.mean(
        weighted * values, axis=-1, keepdims=True
    )
    return grad_values


def dot(a, b):
    return jnp.dot(a, b, preferred_element_type=F32)


def per_device(
    tokens, prefix_len, w_qkv, w_out, w_up, w_down, conv_w, gain_attn, gain_ffn, cotangent
):
    blocks = lax.axis_size("seq")
    me = lax.axis_index("seq")
    rows, width = tokens.shape[1:]
    own = HEADS // blocks * HEAD_DIM
    depth = w_qkv.shape[0]

    shards, copies = lax.axis_size("shard"), lax.axis_size("replica")
    heads = HEADS // blocks
    columns = w_qkv.reshape(depth, 3, blocks, heads, HEAD_DIM).transpose(2, 0, 3, 1, 4)
    gains = jnp.pad(jnp.stack([gain_attn, gain_ffn]), ((0, 0), (0, conv_w.shape[1] - depth)))
    small = jnp.pad(jnp.concatenate([gains, conv_w]), ((0, 3), (0, 0)))
    normed_all, projected, small, full_qkv, full_out, full_up = gather_all(
        tokens[0], small, columns.reshape(blocks, depth, 3 * own), w_out, w_up, blocks, shards
    )
    full_qkv = full_qkv.reshape(blocks, width, 3 * own)
    full_out = full_out.reshape(width, width)
    full_up = full_up.reshape(width, -1)
    full_gone = small[:, 0, 0, :depth].reshape(width).astype(F32)
    full_gtwo = small[:, 0, 1, :depth].reshape(width).astype(F32)
    full_conv = small[:, 0, 2:5].transpose(1, 0, 2)
    own_conv = lax.dynamic_index_in_dim(full_conv.reshape(3, 3, blocks, heads, HEAD_DIM), me, 2, False)
    own_conv = own_conv.transpose(2, 0, 1, 3).reshape(heads, 3, 3 * HEAD_DIM).astype(F32)
    attended_own, logsum, attended, full_down = attention_fwd(
        prefix_len, projected, own_conv, w_down.reshape(-1, depth, width), blocks, shards
    )
    full_down = full_down.reshape(-1, width)
    attended = attended.reshape(width, rows)

    inputs = tokens[0].astype(F32)
    scale_one = rms_scale(inputs)
    hidden = inputs + tn(attended, full_out)
    scale_two = rms_scale(hidden)
    normed_two_b = (hidden * scale_two * full_gtwo).astype(BF)
    positive = jnp.maximum(dot(normed_two_b, full_up), 0.0)
    active_b = (positive * positive).astype(BF)
    output = hidden + dot(active_b, full_down)

    incoming = cotangent[0]
    grad_upper_b = (dot(incoming, full_down.T) * 2.0 * positive).astype(BF)
    grad_normed_two = dot(grad_upper_b, full_up.T)
    grad_hidden = incoming.astype(F32) + norm_back(hidden, scale_two, full_gtwo, grad_normed_two)
    grad_hidden_b = grad_hidden.astype(BF)
    grad_attended = nt(full_out, grad_hidden_b).astype(BF)

    mine = depth // 8

    def cut(grad):
        return grad.astype(BF).reshape(shards // 2, 2, -1, mine, 8, width)

    parts = [
        cut(dot(normed_two_b.T, grad_upper_b[:, i * width : (i + 1) * width]))
        for i in range(grad_upper_b.shape[1] // width)
    ]
    parts += [cut(dot(active_b.T, incoming)), cut(dot(attended, grad_hidden_b))]
    pieces = sum(part.shape[2] for part in parts)
    if mine % (copies * blocks):
        units = -(-pieces * mine // (copies * blocks)) * copies * blocks
        joined = [part.reshape(shards // 2, 2, -1, 8, width) for part in parts]
        joined.append(jnp.zeros((shards // 2, 2, units - pieces * mine, 8, width), BF))
        joined = jnp.concatenate(joined, axis=2)
        parts = [joined.reshape(shards // 2, 2, -1, copies * blocks, 8, width)]

    grad_projected, sums, own_sums = attention_bwd(
        prefix_len, projected, own_conv, grad_attended.reshape(HEADS, HEAD_DIM, rows),
        attended_own, logsum, normed_all, parts, {"replica": copies},
    )
    grad_projected = grad_projected.reshape(blocks, 3 * own, rows)
    grad_normed = sum(
        lax.dot_general(
            grad_projected[j], full_qkv[j], (((0,), (1,)), ((), ())), preferred_element_type=F32
        )
        for j in range(blocks)
    )
    grad_input = (grad_hidden + norm_back(inputs, scale_one, full_gone, grad_normed)).astype(BF)

    sums = sums.reshape(-1, 8, width)[: pieces * mine].reshape(pieces, depth, width)
    ups = w_up.shape[1] // width
    total_up = jnp.concatenate(list(sums[:ups]), axis=1).astype(F32)
    total_down = sums[ups:-1].reshape(-1, width).astype(F32)
    total_out = sums[-1].astype(F32)

    def merge(array):
        array = array.reshape(heads, blocks, -1, 3, HEAD_DIM).transpose(2, 3, 1, 0, 4)
        return array.reshape(array.shape[0], -1).astype(F32)

    total_qkv = merge(own_sums[:, :, :mine].reshape(heads, blocks, depth, -1))
    total_conv = merge(own_sums[:, :, mine, :3])
    at = lax.axis_index("shard")

    def gain_grad(grad, weight, gain):
        return jnp.sum(grad * weight.astype(F32), axis=1) / gain.astype(F32)

    return (
        output[None].astype(BF),
        grad_input[None],
        total_qkv,
        total_out,
        total_up,
        total_down,
        lax.dynamic_slice_in_dim(total_conv, at * conv_w.shape[1], conv_w.shape[1], 1),
        gain_grad(total_qkv, w_qkv, gain_attn),
        gain_grad(total_up, w_up, gain_ffn),
    )


def solution(mesh):
    placed = (
        P(("shard", "replica"), "seq", None),
        P(("shard", "replica")),
        P("shard", None),
        P("shard", None),
        P("shard", None),
        P("shard", None),
        P(None, "shard"),
        P("shard"),
        P("shard"),
        P(("shard", "replica"), "seq", None),
    )
    return jax.shard_map(
        per_device,
        mesh=mesh,
        in_specs=placed,
        out_specs=(
            P(("shard", "replica"), "seq", None),
            P(("shard", "replica"), "seq", None),
            P("shard", None),
            P("shard", None),
            P("shard", None),
            P("shard", None),
            P(None, "shard"),
            P("shard"),
            P("shard"),
        ),
        check_vma=False,
    )
```

profile of v0, /device:TPU:0, one launch (start us, length us, event | category | flops | bytes accessed | tf_op | source)
XLA Modules:
  0.0 331.6 jit_solution(4876308724895001819)
XLA Ops:
  2.6 1.3 fusion.20.small_ref
  3.9 1.5 copy.34
  5.6 1.3 copy.36.qkv_ref
  6.9 68.7 %gather_all.1 = (bf16[768,2048]{1,0:T(8,128)(2,1)}, bf16[2048,576]{1,0:T(8,128)(2,1)}, bf16[4,1,8,576]{3,2,1,0:T(8,128)(2,1)}, bf16[4,4,192,576]{3,2,1,0:T(8,128...) custom-call(bf16[512,768]{1,0:T(8,128)(2,1)} %bitcast.103, ...), custom_call_target="tpu_custom_call" | custom-call | tf_op jit(solution)/shard_map/gather_all/pallas_call | solution.py:280
  75.7 0.8 convert_reduce_fusion
  78.9 4.1 %fusion.26 = (bf16[1,4,192,576]{3,2,1,0:T(8,128)(2,1)}, bf16[1,4,192,576]{3,2,1,0:T(8,128)(2,1)}, bf16[1,4,192,576]{3,2,1,0:T(8,128)(2,1)}, bf16[1,4,192,576]{3,2,1,0:T(8,128)(2,1)}) fusion(bf16[4,4,192,576]{3,2,1,0:T(8,128)(2,1)} %get-tuple-element.32), kind=kLoop, calls=%fused_computation.72 | loop fusion | bytes 7077888 | tf_op jit(solution)/shard_map/slice | solution.py:937
  83.0 39.0 %attention_fwd.1 = (bf16[3,4,64,512]{3,2,1,0:T(8,128)(2,1)}, f32[3,8,2048]{2,1,0:T(8,128)}, bf16[12,64,512]{2,1,0:T(8,128)(2,1)}, bf16[4,4,192,768]{3,2,1,0:T(8,128)(2,1)}) custom-call(s32[1]{0:T(128)S(6)} %copy.46.prefix_ref.refs_0_, bf16[2048,576]{1,0:T(8,128)(2,1)} %get-tuple-element.22.proj_ref.refs_1_, f32[3,3,192]{2,1,0:T(4,128)} %reshape.184.conv_ref.refs_2_, ...), custom_call_target="tpu_custom_call" | custom-call | flops 3221225472 | bytes 2359296 | tf_op jit(solution)/shard_map/attention_fwd/pallas_call | solution.py:376
  122.1 2.2 multiply_reduce_fusion.3
  124.6 2.6 fusion.28
  127.3 3.6 %fusion.7 = bf16[1,512,768]{2,1,0:T(8,128)(2,1)} fusion(f32[512,768]{1,0:T(8,128)S(1)} %get-tuple-element.77, bf16[3072,768]{1,0:T(8,128)(2,1)S(1)} %bitcast.127, f32[512,3072]{1,0:T(8,128)S(1)} %fusion.28), kind=kOutput, calls=%fused_computation.29 | convolution fusion | flops 2421424128 | bytes 13369344 | tf_op jit(solution)/shard_map/dot_general | solution.py:862
  130.9 2.9 fusion
  133.8 2.8 multiply_reduce_fusion.2
  136.6 4.5 %convolution_convert_fusion = bf16[3072,768]{1,0:T(8,128)(2,1)} fusion(f32[512,3072]{1,0:T(8,128)S(1)} %fusion.28, bf16[1,512,768]{2,1,0:T(8,128)(2,1)S(1)} %copy-done.16), kind=kOutput, calls=%fused_computation.3 | convolution fusion | flops 2422996992 | bytes 11796480 | tf_op jit(solution)/shard_map/dot_general | solution.py:862
  141.5 1.7 convolution_convert_fusion.6
  143.2 1.9 convolution_convert_fusion.1
  145.1 1.8 convolution_convert_fusion.2
  146.9 1.8 convolution_convert_fusion.3
  148.8 1.8 convolution_convert_fusion.4
  150.6 1.8 convolution_convert_fusion.5
  152.4 151.1 %attention_bwd.1 = (bf16[12,192,512]{2,1,0:T(8,128)(2,1)}, bf16[9,24,8,768]{3,2,1,0:T(8,128)(2,1)}, bf16[3,4,26,8,192]{4,3,2,1,0:T(8,128)(2,1)}) custom-call(s32[1]{0:T(128)S(6)} %copy.46.prefix_ref.refs_0_, bf16[2048,576]{1,0:T(8,128)(2,1)} %get-tuple-element.22.proj_ref.refs_1_, f32[3,3,192]{2,1,0:T(4,128)} %reshape.184.conv_ref.refs_2_, ...), custom_call_target="tpu_custom_call" | custom-call | flops 8053063680 | bytes 1572864 | tf_op jit(solution)/shard_map/attention_bwd/pallas_call | solution.py:822
  303.6 2.9 fusion.27
  309.0 2.0 fusion.30
  311.1 0.8 fusion.29
  312.5 1.2 fusion.1
  313.9 1.3 fusion.8
  315.5 1.5 copy-done.12
  317.1 0.9 slice_bitcast_fusion.3
  318.0 1.7 bitcast_convert_fusion
  319.7 1.7 multiply_reduce_fusion
  321.4 3.2 reshape.192
  324.6 3.8 %copy.40 = f32[192,3,4,3,64]{0,4,3,2,1:T(8,128)S(1)} copy(f32[192,3,4,3,64]{4,1,0,2,3:T(4,128)} %bitcast.101) | data formatting | bytes 3538944 | tf_op jit(solution)/shard_map/convert_element_type | solution.py:951
  328.8 1.8 copy.44
  (74 shorter events, 9.2 us)
Async XLA Ops:
  5.5 1.5 copy-start.2
  83.0 39.0 %copy-start.4 = (bf16[1,512,768]{2,1,0:T(8,128)(2,1)S(1)}, bf16[1,512,768]{2,1,0:T(8,128)(2,1)}, u32[]{:S(2)}) copy-start(bf16[1,512,768]{2,1,0:T(8,128)(2,1)} %param.10) | copy-start | bytes 2359300
  83.0 39.0 %copy-start.20 = (bf16[4,1,192,768]{3,2,1,0:T(8,128)(2,1)S(1)}, bf16[4,1,192,768]{3,2,1,0:T(8,128)(2,1)}, u32[]{:S(2)}) copy-start(bf16[4,1,192,768]{3,2,1,0:T(8,128)(2,1)} %get-tuple-element.25) | copy-start | bytes 3538948
  122.1 2.6 copy-start.7
  124.3 3.0 slice-start
  124.6 2.6 slice-start.1
  127.3 3.6 %copy-start.16 = (bf16[1,512,768]{2,1,0:T(8,128)(2,1)S(1)}, bf16[1,512,768]{2,1,0:T(8,128)(2,1)}, u32[]{:S(2)}) copy-start(bf16[1,512,768]{2,1,0:T(8,128)(2,1)} %param.19) | copy-start | bytes 2359300
  141.5 1.7 copy-start
  141.5 1.7 copy-start.15
  303.6 2.9 copy-start.11
  306.5 2.6 copy-start.10
  309.0 2.0 copy-start.9
  309.0 2.0 copy-start.13
  311.1 1.1 copy-start.5
  311.1 1.4 copy-start.8
  311.1 1.4 copy-start.17
  312.5 1.4 copy-start.1
  313.9 1.3 copy-start.14
  315.2 1.7 copy-start.12
  318.0 1.7 copy-start.6
  324.5 3.8 %copy-start.3 = (bf16[192,2304]{0,1:T(8,128)(2,1)S(1)}, bf16[192,2304]{0,1:T(8,128)(2,1)}, u32[]{:S(2)}) copy-start(bf16[192,2304]{0,1:T(8,128)(2,1)} %copy-done.2) | copy-start | bytes 2654212
  328.7 1.8 copy-start.18
  328.7 1.8 copy-start.19
where the time goes:
time: 338 us; the launch traced here: 332 us
  Pallas kernels  259 us (77%)
  matrix products  34.4 us (10%)
  local copies, waits for them, and re-layouts  25.9 us (8%)
  other arithmetic  10.3 us (3%)
    pallas_call x1, Pallas kernels, attention_bwd(): pl.pallas_call(functools.partial(bwd_kernel, counts), out_shape=(jax.Shap...  151 us
    pallas_call x1, Pallas kernels, gather_all(): pl.pallas_call(gather_kernel, out_shape=[jax.ShapeDtypeStruct((width, blo...  68.7 us
    pallas_call x1, Pallas kernels, attention_fwd(): pl.pallas_call(fwd_kernel, out_shape=(jax.ShapeDtypeStruct(own, BF), jax....  39 us
    dot_general x10, matrix products, dot(): return jnp.dot(a, b, preferred_element_type=F32)  25.6 us
    convert_element_type x6, local copies, waits for them, and re-layouts, merge(): return array.reshape(array.shape[0], -1).astype(F32)  7.24 us

commit v1 on v0

--- a/solution.py
+++ b/solution.py
@@ -151,7 +151,7 @@
 def gather_kernel(
     tok_ref, small_ref, qkv_ref, out_ref, up_ref,
     normed_ref, proj_ref, small_all, qkv_all, out_all, up_all,
-    toks, sl, sr, rl, rr, *sems,
+    toks, weight_s, wsem, sl, sr, rl, rr, *sems,
 ):
     blocks, rows, width = toks.shape
     _, shards, depth, columns = qkv_all.shape
@@ -195,7 +195,10 @@
     qkv.own().wait()
     qkv.arrive(z)
     gain = jnp.concatenate([small_all[s, 0, 0:1, :depth] for s in range(shards)], axis=1).astype(F32)
-    weight = qkv_all[z].reshape(shards * depth, columns)
+    fetch = pltpu.make_async_copy(qkv_all.at[z], weight_s, wsem.at[0])
+    fetch.start()
+    fetch.wait()
+    weight = weight_s[...].reshape(shards * depth, columns)
 
     def project(b, values):
         at = pl.ds(pl.multiple_of(b * rows, rows), rows)
@@ -290,8 +293,9 @@
             for i, array in enumerate(arrays)
         ],
         in_specs=[vm] * 5,
-        out_specs=[vm] * 4 + [hbm] * 2,
-        scratch_shapes=[pltpu.VMEM((blocks, rows, width), BF)] + sems,
+        out_specs=[vm] * 3 + [hbm] * 3,
+        scratch_shapes=[pltpu.VMEM((blocks, rows, width), BF), pltpu.VMEM((shards,) + qkv.shape[1:], BF), dma((1,))]
+        + sems,
         compiler_params=pltpu.CompilerParams(
             vmem_limit_bytes=60 * 1024 * 1024, collective_id=4, has_side_effects=True
         ),
@@ -532,10 +536,11 @@
         for i in range(1, self.nx):
             self.copy_f(k, i, True).start()
 
+    LAGS = (0, 1, 3, 5, 7, 9)
+
     def step(self, t):
-        for lag, stage in enumerate(
-            (self.stage_c, self.stage_d, self.stage_near, self.stage_far, self.stage_back, self.stage_f)
-        ):
+        stages = (self.stage_c, self.stage_d, self.stage_near, self.stage_far, self.stage_back, self.stage_f)
+        for lag, stage in zip(self.LAGS, stages):
             @pl.when((t >= lag) & (t < self.chunks + lag))
             def _():
                 stage(t - lag)
@@ -698,6 +703,9 @@
     def gp_copy(h, i, at):
         return remote(gpt.at[h, i], gp_ref.at[at * heads + h], gsend.at[h, i], grecv.at[h, at], (i, 2 * y + c, x))
 
+    ahead = min(2, sums.chunks)
+    for k in range(ahead):
+        sums.stage_b(k)
     convolve(proj_ref, conv_ref, wide, (qs, ks, vs))
 
     def head(h, _):
@@ -710,13 +718,15 @@
         dq[...] = jnp.zeros(dq.shape, F32)
         def kblock(j, _):
             t = h*blocks + j
-            @pl.when(t < sums.chunks)
+            @pl.when(t + ahead < sums.chunks)
             def _():
-                sums.stage_b(t)
-            turn = (2*t)//3
-            @pl.when((turn > 0) & ((2*t)%3 != 2))
+                sums.stage_b(t + ahead)
+            @pl.when((t > 0) & (t != 3))
             def _():
-                sums.step(turn - 1)
+                sums.step(jnp.where(t < 3, t - 1, t - 2))
+            @pl.when((h > 0) & (j > 0))
+            def _():
+                gp_copy(h - 1, (z + j) % blocks, z).start()
             for n, stage in enumerate(own.stages()):
                 @pl.when((h > 0) & (j == n))
                 def _():
@@ -759,9 +769,6 @@
             gp = taps[0:1]*g0 + taps[1:2]*g[1:rows+1] + taps[2:3]*g[2:rows+2]
             gp_s[pl.ds(base, rows)] = gp.astype(BF)
             gpt[h, i] = jnp.transpose(gp).astype(BF)
-            @pl.when(i != z)
-            def _():
-                gp_copy(h, i, z).start()
             add = [jnp.sum(g0*w[8-t:8-t+rows], axis=0, keepdims=True) for t in range(3)]
             return tuple(a+b for a, b in zip(total, add))
         total = lax.fori_loop(0, blocks, out, tuple(jnp.zeros((1, width), F32) for _ in range(3)))
@@ -779,19 +786,23 @@
     gwide[length:length+8] = jnp.zeros((8, width), F32)
     lax.fori_loop(0, heads, head, 0)
     steps = heads*blocks
-    turns = (2*(steps - 1))//3
+    turns = steps - 2
     def rest(t, _):
         sums.stage_b(t)
         return 0
-    lax.fori_loop(steps, sums.chunks, rest, 0)
+    lax.fori_loop(steps + ahead, sums.chunks, rest, 0)
     for n, stage in enumerate(own.stages()):
         sums.step(turns + n)
+        if 0 < n < blocks:
+            gp_copy(heads - 1, (z + n) % blocks, z).start()
         stage(heads - 1)
     count = len(own.stages())
+    for n in range(count, blocks):
+        gp_copy(heads - 1, (z + n) % blocks, z).start()
     def tail(t, _):
         sums.step(t)
         return 0
-    lax.fori_loop(turns + count, max(sums.chunks + 5, turns + count), tail, 0)
+    lax.fori_loop(turns + count, max(sums.chunks + sums.LAGS[-1], turns + count), tail, 0)
     sums.finish()
     def done(h, _):
         own.finish(h)
@@ -846,6 +857,105 @@
     )(prefix, proj, conv, do, o, lse, normed, *parts)
 
 
+def finish_kernel(
+    gp_ref, sum_ref, own_ref, wq_ref, tok_ref, gh_ref, gone_ref, w_qkv_ref, w_up_ref, gains_ref,
+    gin_out, qkv_out, out_out, up_out, down_out, conv_ref, ggain_ref,
+    wq, tok, gh, w_qkv, w_up, gin, qkv, out, up, down, isem, osem,
+):
+    depth = w_qkv.shape[0]
+    width = tok.shape[1]
+    heads, blocks = own_ref.shape[:2]
+    mine = depth // 8
+    loads = [
+        pltpu.make_async_copy(src, dst, isem.at[i])
+        for i, (src, dst) in enumerate(
+            ((wq_ref, wq), (tok_ref, tok), (gh_ref, gh), (w_up_ref, w_up), (w_qkv_ref, w_qkv))
+        )
+    ]
+    for load in loads:
+        load.start()
+    stores = [
+        pltpu.make_async_copy(src, dst, osem.at[i])
+        for i, (src, dst) in enumerate(
+            ((down, down_out), (out, out_out), (up, up_out), (qkv, qkv_out), (gin, gin_out))
+        )
+    ]
+    ups = w_up.shape[1] // width
+    downs = down.shape[0] // depth
+
+    def rows_of(first, count):
+        return sum_ref[first * mine : (first + count) * mine].reshape(count * depth, width).astype(F32)
+
+    for i in range(downs):
+        down[i * depth : (i + 1) * depth] = rows_of(ups + i, 1)
+    stores[0].start()
+    out[...] = rows_of(ups + downs, 1)
+    stores[1].start()
+    loads[3].wait()
+    total = jnp.zeros((depth, 1), F32)
+    for i in range(ups):
+        at = slice(i * width, (i + 1) * width)
+        grad = rows_of(i, 1)
+        up[:, at] = grad
+        total = total + jnp.sum(grad * w_up[:, at].astype(F32), axis=1, keepdims=True)
+    stores[2].start()
+    grads = [own_ref[h, j, :mine].reshape(depth, 3 * HEAD_DIM) for j in range(blocks) for h in range(heads)]
+    taps = [own_ref[h, j, mine] for j in range(blocks) for h in range(heads)]
+
+    def merge(pieces, p):
+        return jnp.concatenate([piece[:, p * HEAD_DIM : (p + 1) * HEAD_DIM] for piece in pieces], axis=1)
+
+    loads[4].wait()
+    attn = jnp.zeros((depth, 1), F32)
+    for p in range(3):
+        at = slice(p * width, (p + 1) * width)
+        grad = merge(grads, p).astype(F32)
+        qkv[:, at] = grad
+        attn = attn + jnp.sum(grad * w_qkv[:, at].astype(F32), axis=1, keepdims=True)
+        conv_ref[:, at] = merge(taps, p).astype(F32)
+    stores[3].start()
+    gains = gains_ref[...]
+    ggain_ref[...] = jnp.concatenate([attn / gains[:, 0:1], total / gains[:, 1:2]], axis=1)
+    for load in loads[:3]:
+        load.wait()
+    e1 = jnp.zeros(gh.shape, F32)
+    for j in range(blocks):
+        e1 = e1 + lax.dot_general(gp_ref[j], wq[j], (((0,), (1,)), ((), ())), preferred_element_type=F32)
+    x = tok[...].astype(F32)
+    scale = lax.rsqrt(jnp.mean(x * x, axis=-1, keepdims=True) + 1e-06)
+    weighted = e1 * gone_ref[...]
+    back = scale * weighted - x * scale**3 * jnp.mean(weighted * x, axis=-1, keepdims=True)
+    gin[...] = (gh[...] + back).astype(BF)
+    stores[4].start()
+    for store in stores:
+        store.wait()
+
+
+def finish(gp, sums, own_sums, wq, tok, gh, gone, w_qkv, w_up, gains, ff):
+    depth, width = w_qkv.shape[0], tok.shape[1]
+    vm = pl.BlockSpec(memory_space=pltpu.VMEM)
+    hbm = pl.BlockSpec(memory_space=pl.ANY)
+    dma = pltpu.SemaphoreType.DMA
+    outs = [
+        (tok.shape, BF),
+        (w_qkv.shape, F32),
+        ((depth, width), F32),
+        (w_up.shape, F32),
+        ((ff, width), F32),
+    ]
+    flat = [((8, w_qkv.shape[1]), F32), ((depth, 2), F32)]
+    kept = [(a.shape, a.dtype) for a in (wq, tok, gh, w_qkv, w_up)]
+    return pl.pallas_call(
+        finish_kernel,
+        out_shape=[jax.ShapeDtypeStruct(*o) for o in outs + flat],
+        in_specs=[vm] * 3 + [hbm] * 3 + [vm] + [hbm] * 2 + [vm],
+        out_specs=[hbm] * 5 + [vm] * 2,
+        scratch_shapes=[pltpu.VMEM(*o) for o in kept + outs] + [dma((5,)), dma((5,))],
+        compiler_params=pltpu.CompilerParams(vmem_limit_bytes=60 * 1024 * 1024),
+        name="finish",
+    )(gp, sums, own_sums, wq, tok, gh, gone, w_qkv, w_up, gains)
+
+
 def rms_scale(values):
     return lax.rsqrt(jnp.mean(values * values, axis=-1, keepdims=True) + 1e-06)
 
@@ -894,7 +1004,6 @@
     attended = attended.reshape(width, rows)
 
     inputs = tokens[0].astype(F32)
-    scale_one = rms_scale(inputs)
     hidden = inputs + tn(attended, full_out)
     scale_two = rms_scale(hidden)
     normed_two_b = (hidden * scale_two * full_gtwo).astype(BF)
@@ -932,31 +1041,13 @@
         attended_own, logsum, normed_all, parts, {"replica": copies},
     )
     grad_projected = grad_projected.reshape(blocks, 3 * own, rows)
-    grad_normed = sum(
-        lax.dot_general(
-            grad_projected[j], full_qkv[j], (((0,), (1,)), ((), ())), preferred_element_type=F32
-        )
-        for j in range(blocks)
+    sums = sums.reshape(-1, 8, width)
+    gains = jnp.stack([gain_attn, gain_ffn], axis=1).astype(F32)
+    grad_input, total_qkv, total_out, total_up, total_down, total_conv, grad_gains = finish(
+        grad_projected, sums, own_sums, full_qkv, tokens[0], grad_hidden, full_gone[None],
+        w_qkv, w_up, gains, w_down.shape[0],
     )
-    grad_input = (grad_hidden + norm_back(inputs, scale_one, full_gone, grad_normed)).astype(BF)
-
-    sums = sums.reshape(-1, 8, width)[: pieces * mine].reshape(pieces, depth, width)
-    ups = w_up.shape[1] // width
-    total_up = jnp.concatenate(list(sums[:ups]), axis=1).astype(F32)
-    total_down = sums[ups:-1].reshape(-1, width).astype(F32)
-    total_out = sums[-1].astype(F32)
-
-    def merge(array):
-        array = array.reshape(heads, blocks, -1, 3, HEAD_DIM).transpose(2, 3, 1, 0, 4)
-        return array.reshape(array.shape[0], -1).astype(F32)
-
-    total_qkv = merge(own_sums[:, :, :mine].reshape(heads, blocks, depth, -1))
-    total_conv = merge(own_sums[:, :, mine, :3])
     at = lax.axis_index("shard")
-
-    def gain_grad(grad, weight, gain):
-        return jnp.sum(grad * weight.astype(F32), axis=1) / gain.astype(F32)
-
     return (
         output[None].astype(BF),
         grad_input[None],
@@ -964,9 +1055,9 @@
         total_out,
         total_up,
         total_down,
-        lax.dynamic_slice_in_dim(total_conv, at * conv_w.shape[1], conv_w.shape[1], 1),
-        gain_grad(total_qkv, w_qkv, gain_attn),
-        gain_grad(total_up, w_up, gain_ffn),
+        lax.dynamic_slice_in_dim(total_conv[:3], at * conv_w.shape[1], conv_w.shape[1], 1),
+        grad_gains[:, 0],
+        grad_gains[:, 1],
     )
 
 

time: 338 us -> 352 us (1.041); the launches traced: 332 us -> 350 us
  Pallas kernels: 259 us -> 301 us
  local copies, waits for them, and re-layouts: 25.9 us -> 12.8 us
  other arithmetic: 10.3 us -> 3.4 us
    pallas_call x1, Pallas kernels: 151 us -> 181 us  [attention_bwd(): pl.pallas_call(functools.partial(bwd_kernel, counts), out_shape=(jax.Shap...]
    pallas_call x0 -> x1, Pallas kernels: none -> 12.8 us  [finish(): pl.pallas_call(finish_kernel, out_shape=[jax.ShapeDtypeStruct(*o) for o i...]
    convert_element_type x6 -> x1, local copies, waits for them, and re-layouts: 7.24 us -> 0.78 us  [per_device(): gains = jnp.stack([gain_attn, gain_ffn], axis=1).astype(F32)]
    dot_general x4 -> x0, matrix products: 4.86 us -> none  [per_device(): lax.dot_general(grad_projected[j], full_qkv[j], (((0,), (1,)), ((), ())),...]
    slice x3 -> x2, local copies, waits for them, and re-layouts: 7.09 us -> 2.64 us  [the longest x1 1.75 us: per_device(): grad_gains[:, 1]]
    unnamed x48 -> x19, local copies, waits for them, and re-layouts: 5.82 us -> 1.55 us
where the time goes in v1:
time: 352 us; the launch traced here: 350 us
  Pallas kernels  301 us (86%)
  matrix products  31.2 us (9%)
  local copies, waits for them, and re-layouts  12.8 us (4%)
    pallas_call x1, Pallas kernels, attention_bwd(): pl.pallas_call(functools.partial(bwd_kernel, counts), out_shape=(jax.Shap...  181 us
    pallas_call x1, Pallas kernels, gather_all(): pl.pallas_call(gather_kernel, out_shape=[jax.ShapeDtypeStruct((width, blo...  67.6 us
    pallas_call x1, Pallas kernels, attention_fwd(): pl.pallas_call(fwd_kernel, out_shape=(jax.ShapeDtypeStruct(own, BF), jax....  39 us
    dot_general x10, matrix products, dot(): return jnp.dot(a, b, preferred_element_type=F32)  27.5 us
    pallas_call x1, Pallas kernels, finish(): pl.pallas_call(finish_kernel, out_shape=[jax.ShapeDtypeStruct(*o) for o i...  12.8 us

profile of v1, /device:TPU:0, one launch (start us, length us, event | category | flops | bytes accessed | tf_op | source)
XLA Modules:
  0.0 349.7 jit_solution(8301890052895709792)
XLA Ops:
  1.3 0.7 stack.19
  1.9 0.7 stack.18
  2.6 1.3 fusion.13.small_ref
  3.9 1.5 copy.36
  5.6 1.3 copy.38.qkv_ref
  6.9 67.6 %gather_all.1 = (bf16[768,2048]{1,0:T(8,128)(2,1)}, bf16[2048,576]{1,0:T(8,128)(2,1)}, bf16[4,1,8,576]{3,2,1,0:T(8,128)(2,1)}, bf16[4,4,192,576]{3,2,1,0:T(8,128...) custom-call(bf16[512,768]{1,0:T(8,128)(2,1)} %bitcast.69, ...), custom_call_target="tpu_custom_call" | custom-call | tf_op jit(solution)/shard_map/gather_all/pallas_call | solution.py:283
  74.5 0.8 slice_bitcast_fusion
  75.5 0.7 reshape.137.conv_ref.refs_2_
  76.2 39.0 %attention_fwd.1 = (bf16[3,4,64,512]{3,2,1,0:T(8,128)(2,1)}, f32[3,8,2048]{2,1,0:T(8,128)}, bf16[12,64,512]{2,1,0:T(8,128)(2,1)}, bf16[4,4,192,768]{3,2,1,0:T(8,128)(2,1)}) custom-call(s32[1]{0:T(128)S(6)} %copy.44.prefix_ref.refs_0_, bf16[2048,576]{1,0:T(8,128)(2,1)} %get-tuple-element.29.proj_ref.refs_1_, f32[3,3,192]{2,1,0:T(4,128)} %reshape.137.conv_ref.refs_2_, ...), custom_call_target="tpu_custom_call" | custom-call | flops 3221225472 | bytes 2359296 | tf_op jit(solution)/shard_map/attention_fwd/pallas_call | solution.py:380
  115.2 2.1 multiply_reduce_fusion.1
  117.3 1.4 convert_reduce_fusion
  119.0 4.6 %fusion.19 = f32[512,3072]{1,0:T(8,128)S(1)} fusion(bf16[512,768]{1,0:T(8,128)(2,1)S(1)} %multiply_convert_fusion.1, bf16[768,3072]{1,0:T(8,128)(2,1)} %bitcast.63), kind=kOutput, calls=%fused_computation.48 | convolution fusion | flops 2415919104 | bytes 11796480 | tf_op jit(solution)/shard_map/dot_general | solution.py:972
  123.7 3.5 %fusion.1 = bf16[1,512,768]{2,1,0:T(8,128)(2,1)} fusion(f32[512,768]{1,0:T(8,128)S(1)} %get-tuple-element.56, bf16[3072,768]{1,0:T(8,128)(2,1)S(1)} %bitcast.83, f32[512,3072]{1,0:T(8,128)S(1)} %fusion.19), kind=kOutput, calls=%fused_computation.17 | convolution fusion | flops 2421424128 | bytes 13369344 | tf_op jit(solution)/shard_map/dot_general | solution.py:972
  127.2 3.1 fusion
  130.3 2.7 multiply_reduce_fusion
  133.1 0.4 subtract_add_fusion.gh_ref
  133.6 1.7 convolution_convert_fusion.6
  135.2 1.8 convolution_convert_fusion.5
  137.1 1.8 convolution_convert_fusion.4
  138.9 1.8 convolution_convert_fusion.3
  140.7 1.8 convolution_convert_fusion.2
  142.5 4.3 %convolution_convert_fusion = bf16[3072,768]{1,0:T(8,128)(2,1)} fusion(f32[512,3072]{1,0:T(8,128)S(1)} %fusion.19, bf16[1,512,768]{2,1,0:T(8,128)(2,1)S(1)} %copy-done.3), kind=kOutput, calls=%fused_computation.3 | convolution fusion | flops 2422996992 | bytes 11796480 | tf_op jit(solution)/shard_map/dot_general | solution.py:972
  146.9 1.9 convolution_convert_fusion.1
  148.8 181.4 %attention_bwd.1 = (bf16[12,192,512]{2,1,0:T(8,128)(2,1)}, bf16[9,24,8,768]{3,2,1,0:T(8,128)(2,1)}, bf16[3,4,26,8,192]{4,3,2,1,0:T(8,128)(2,1)}) custom-call(s32[1]{0:T(128)S(6)} %copy.44.prefix_ref.refs_0_, bf16[2048,576]{1,0:T(8,128)(2,1)} %get-tuple-element.29.proj_ref.refs_1_, f32[3,3,192]{2,1,0:T(4,128)} %reshape.137.conv_ref.refs_2_, ...), custom_call_target="tpu_custom_call" | custom-call | flops 8053063680 | bytes 1572864 | tf_op jit(solution)/shard_map/attention_bwd/pallas_call | solution.py:833
  330.1 1.4 reshape.139.gone_ref
  331.5 0.7 stack.22
  332.2 0.7 stack.21
  332.8 0.8 copy.42.gains_ref
  333.6 12.8 %finish.1 = (bf16[512,768]{1,0:T(8,128)(2,1)}, f32[192,2304]{1,0:T(8,128)}, f32[192,768]{1,0:T(8,128)}, f32[192,3072]{1,0:T(8,128)}, f32[768,768]{1,0:T(8,128)}, /*index=5*/f32[8,2304]{1,0:T(8,128)}, f32[192,2]{1,0:T(8,128)}) custom-call(bf16[4,576,512]{2,1,0:T(8,128)(2,1)} %bitcast.72, bf16[216,8,768]{2,1,0:T(8,128)(2,1)} %bitcast.71, ...), custom_call_target="tpu_custom_call" | custom-call | tf_op jit(solution)/shard_map/finish/pallas_call | solution.py:948
  346.4 0.9 slice.37
  347.3 0.7 constant_dynamic-slice_fusion
  347.9 1.8 slice_reduce_fusion
  (31 shorter events, 0.6 us)
Async XLA Ops:
  76.2 39.0 %copy-start.1 = (bf16[1,512,768]{2,1,0:T(8,128)(2,1)S(1)}, bf16[1,512,768]{2,1,0:T(8,128)(2,1)}, u32[]{:S(2)}) copy-start(bf16[1,512,768]{2,1,0:T(8,128)(2,1)} %param.10) | copy-start | bytes 2359300
  76.2 39.0 %copy-start.4 = (bf16[4,1,192,768]{3,2,1,0:T(8,128)(2,1)S(1)}, bf16[4,1,192,768]{3,2,1,0:T(8,128)(2,1)}, u32[]{:S(2)}) copy-start(bf16[4,1,192,768]{3,2,1,0:T(8,128)(2,1)} %get-tuple-element.32) | copy-start | bytes 3538948
  118.8 4.9 %slice-start.2 = ((s8[4718592]{0:T(1024)(128)(4,1)}), s8[4194304]{0:T(1024)(128)(4,1)S(1)}, s32[]{:S(2)}) async-start(s8[4718592]{0:T(1024)(128)(4,1)} %bitcast.81), calls=%async_computation.2 | async-start | bytes 8388608
  119.0 4.7 %slice-start.3 = ((s8[4718592]{0:T(1024)(128)(4,1)}), s8[524288]{0:T(1024)(128)(4,1)S(1)}, s32[]{:S(2)}) async-start(s8[4718592]{0:T(1024)(128)(4,1)} %bitcast.81), calls=%async_computation.3 | async-start | bytes 1048576
  123.7 3.6 %copy-start.3 = (bf16[1,512,768]{2,1,0:T(8,128)(2,1)S(1)}, bf16[1,512,768]{2,1,0:T(8,128)(2,1)}, u32[]{:S(2)}) copy-start(bf16[1,512,768]{2,1,0:T(8,128)(2,1)} %param.19) | copy-start | bytes 2359300
  123.7 6.6 %slice-start = ((s8[4718592]{0:T(1024)(128)(4,1)}), s8[4194304]{0:T(1024)(128)(4,1)S(1)}, s32[]{:S(2)}) async-start(s8[4718592]{0:T(1024)(128)(4,1)} %bitcast.64), calls=%async_computation | async-start | bytes 8388608
  127.2 3.1 slice-start.1
  133.5 13.3 %copy-start = (f32[512,768]{1,0:T(8,128)}, f32[512,768]{1,0:T(8,128)S(1)}, u32[]{:S(2)}) copy-start(f32[512,768]{1,0:T(8,128)S(1)} %subtract_add_fusion.gh_ref) | copy-start | bytes 4718596
  142.5 4.3 %copy-start.2 = (bf16[12,64,512]{2,1,0:T(8,128)(2,1)S(1)}, bf16[12,64,512]{2,1,0:T(8,128)(2,1)}, u32[]{:S(2)}) copy-start(bf16[12,64,512]{2,1,0:T(8,128)(2,1)} %get-tuple-element.31) | copy-start | bytes 2359300

commit v2 on v1

--- a/solution.py
+++ b/solution.py
@@ -536,7 +536,7 @@
         for i in range(1, self.nx):
             self.copy_f(k, i, True).start()
 
-    LAGS = (0, 1, 3, 5, 7, 9)
+    LAGS = (0, 1, 2, 3, 4, 5)
 
     def step(self, t):
         stages = (self.stage_c, self.stage_d, self.stage_near, self.stage_far, self.stage_back, self.stage_f)
@@ -724,10 +724,7 @@
             @pl.when((t > 0) & (t != 3))
             def _():
                 sums.step(jnp.where(t < 3, t - 1, t - 2))
-            @pl.when((h > 0) & (j > 0))
-            def _():
-                gp_copy(h - 1, (z + j) % blocks, z).start()
-            for n, stage in enumerate(own.stages()):
+            for n, stage in enumerate(own.stages()[:3], 1):
                 @pl.when((h > 0) & (j == n))
                 def _():
                     stage(h - 1)
@@ -772,15 +769,22 @@
             add = [jnp.sum(g0*w[8-t:8-t+rows], axis=0, keepdims=True) for t in range(3)]
             return tuple(a+b for a, b in zip(total, add))
         total = lax.fori_loop(0, blocks, out, tuple(jnp.zeros((1, width), F32) for _ in range(3)))
+        @pl.when(h < heads - 1)
+        def _():
+            for i in range(1, blocks):
+                gp_copy(h, (z + i) % blocks, z).start()
         gp_ref[z * heads + h] = gpt[h, z]
         grad = jnp.dot(normed_ref[...], gp_s[...], preferred_element_type=F32).astype(BF)
         shape = own_part.shape[1:]
-        mine = grad.shape[0] // (8 * shape[0] * shape[1])
-        own_part[h, :, :, 0:mine] = grad.reshape(shape[0], shape[1], mine, 8, width)
-        extra = jnp.concatenate(list(total) + [jnp.zeros((5, width), F32)], axis=0).astype(BF)
-        own_part[h, :, :, mine] = jnp.broadcast_to(extra, shape[:2] + (8, width))
+        mine = grad.shape[0] // (16 * shape[0] * shape[1])
+        grad = grad.reshape(shape[0] * shape[1], 2, 8 * mine, width)
+        grad = jnp.concatenate([grad[:, 0], grad[:, 1]], axis=2)
+        own_part[h, :, :, 0:mine] = grad.reshape(shape[0], shape[1], mine, 8, 2 * width)
+        extra = jnp.concatenate(list(total) + [jnp.zeros((5, width), F32)], axis=0)
+        extra = jnp.concatenate([extra, jnp.zeros((8, width), F32)], axis=1).astype(BF)
+        own_part[h, :, :, mine] = jnp.broadcast_to(extra, shape[:2] + (8, 2 * width))
         for spare in range(mine + 1, shape[2]):
-            own_part[h, :, :, spare] = jnp.zeros(shape[:2] + (8, width), BF)
+            own_part[h, :, :, spare] = jnp.zeros(shape[:2] + (8, 2 * width), BF)
         own.copy_a(h).start()
         return 0
     gwide[length:length+8] = jnp.zeros((8, width), F32)
@@ -793,9 +797,11 @@
     lax.fori_loop(steps + ahead, sums.chunks, rest, 0)
     for n, stage in enumerate(own.stages()):
         sums.step(turns + n)
-        if 0 < n < blocks:
-            gp_copy(heads - 1, (z + n) % blocks, z).start()
         stage(heads - 1)
+    def forward(h, _):
+        own.stage_f(h)
+        return 0
+    lax.fori_loop(0, heads - 1, forward, 0)
     count = len(own.stages())
     for n in range(count, blocks):
         gp_copy(heads - 1, (z + n) % blocks, z).start()
@@ -803,6 +809,8 @@
         sums.step(t)
         return 0
     lax.fori_loop(turns + count, max(sums.chunks + sums.LAGS[-1], turns + count), tail, 0)
+    for n in range(1, blocks):
+        gp_copy(heads - 1, (z + n) % blocks, z).start()
     sums.finish()
     def done(h, _):
         own.finish(h)
@@ -825,8 +833,8 @@
     nx = shape["replica"]
     chunks = sum(counts)
     half = units // nx
-    own_units = -(-(normed.shape[0] // (16 * ny) + 1) // nx) * nx
-    own_unit = (8, width)
+    own_units = -(-(normed.shape[0] // (32 * ny) + 1) // nx) * nx
+    own_unit = (8, 2 * width)
     vm = pl.BlockSpec(memory_space=pltpu.VMEM)
     dma = pltpu.SemaphoreType.DMA
     per = pltpu.VMEM((heads, length, HEAD_DIM), BF)
@@ -899,8 +907,14 @@
         up[:, at] = grad
         total = total + jnp.sum(grad * w_up[:, at].astype(F32), axis=1, keepdims=True)
     stores[2].start()
-    grads = [own_ref[h, j, :mine].reshape(depth, 3 * HEAD_DIM) for j in range(blocks) for h in range(heads)]
-    taps = [own_ref[h, j, mine] for j in range(blocks) for h in range(heads)]
+    lanes = 3 * HEAD_DIM
+
+    def grad_of(h, j):
+        pair = own_ref[h, j, : mine // 2].reshape(depth // 2, 2 * lanes)
+        return jnp.concatenate([pair[:, :lanes], pair[:, lanes:]], axis=0)
+
+    grads = [grad_of(h, j) for j in range(blocks) for h in range(heads)]
+    taps = [own_ref[h, j, mine // 2] for j in range(blocks) for h in range(heads)]
 
     def merge(pieces, p):
         return jnp.concatenate([piece[:, p * HEAD_DIM : (p + 1) * HEAD_DIM] for piece in pieces], axis=1)

time: 352 us -> 322 us (0.915)
  Pallas kernels: 301 us -> 271 us
    pallas_call x1, Pallas kernels: 181 us -> 151 us  [attention_bwd(): pl.pallas_call(functools.partial(bwd_kernel, counts), out_shape=(jax.Shap...]
where the time goes in v2:
time: 322 us; the launch traced here: 319 us
  Pallas kernels  271 us (84%)
  matrix products  31.2 us (10%)
  local copies, waits for them, and re-layouts  12.8 us (4%)
  other arithmetic  3.4 us (1%)
    pallas_call x1, Pallas kernels, attention_bwd(): pl.pallas_call(functools.partial(bwd_kernel, counts), out_shape=(jax.Shap...  151 us
    pallas_call x1, Pallas kernels, gather_all(): pl.pallas_call(gather_kernel, out_shape=[jax.ShapeDtypeStruct((width, blo...  67.6 us
    pallas_call x1, Pallas kernels, attention_fwd(): pl.pallas_call(fwd_kernel, out_shape=(jax.ShapeDtypeStruct(own, BF), jax....  39 us
    dot_general x10, matrix products, dot(): return jnp.dot(a, b, preferred_element_type=F32)  27.4 us
    pallas_call x1, Pallas kernels, finish(): pl.pallas_call(finish_kernel, out_shape=[jax.ShapeDtypeStruct(*o) for o i...  12.7 us

profile of v2, /device:TPU:0, one launch (start us, length us, event | category | flops | bytes accessed | tf_op | source)
XLA Modules:
  0.0 319.5 jit_solution(10776455142411039244)
XLA Ops:
  1.3 0.7 stack.19
  1.9 0.7 stack.18
  2.6 1.3 fusion.13.small_ref
  3.9 1.5 copy.36
  5.6 1.3 copy.38.qkv_ref
  6.9 67.6 %gather_all.1 = (bf16[768,2048]{1,0:T(8,128)(2,1)}, bf16[2048,576]{1,0:T(8,128)(2,1)}, bf16[4,1,8,576]{3,2,1,0:T(8,128)(2,1)}, bf16[4,4,192,576]{3,2,1,0:T(8,128...) custom-call(bf16[512,768]{1,0:T(8,128)(2,1)} %bitcast.69, ...), custom_call_target="tpu_custom_call" | custom-call | tf_op jit(solution)/shard_map/gather_all/pallas_call | solution.py:283
  74.5 0.8 slice_bitcast_fusion
  75.5 0.7 reshape.137.conv_ref.refs_2_
  76.2 39.0 %attention_fwd.1 = (bf16[3,4,64,512]{3,2,1,0:T(8,128)(2,1)}, f32[3,8,2048]{2,1,0:T(8,128)}, bf16[12,64,512]{2,1,0:T(8,128)(2,1)}, bf16[4,4,192,768]{3,2,1,0:T(8,128)(2,1)}) custom-call(s32[1]{0:T(128)S(6)} %copy.44.prefix_ref.refs_0_, bf16[2048,576]{1,0:T(8,128)(2,1)} %get-tuple-element.29.proj_ref.refs_1_, f32[3,3,192]{2,1,0:T(4,128)} %reshape.137.conv_ref.refs_2_, ...), custom_call_target="tpu_custom_call" | custom-call | flops 3221225472 | bytes 2359296 | tf_op jit(solution)/shard_map/attention_fwd/pallas_call | solution.py:380
  115.2 2.1 multiply_reduce_fusion.1
  117.3 1.4 convert_reduce_fusion
  119.0 4.6 %fusion.19 = f32[512,3072]{1,0:T(8,128)S(1)} fusion(bf16[512,768]{1,0:T(8,128)(2,1)S(1)} %multiply_convert_fusion.1, bf16[768,3072]{1,0:T(8,128)(2,1)} %bitcast.64), kind=kOutput, calls=%fused_computation.48 | convolution fusion | flops 2415919104 | bytes 11796480 | tf_op jit(solution)/shard_map/dot_general | solution.py:986
  123.7 3.5 %fusion.1 = bf16[1,512,768]{2,1,0:T(8,128)(2,1)} fusion(f32[512,768]{1,0:T(8,128)S(1)} %get-tuple-element.56, bf16[3072,768]{1,0:T(8,128)(2,1)S(1)} %bitcast.83, f32[512,3072]{1,0:T(8,128)S(1)} %fusion.19), kind=kOutput, calls=%fused_computation.17 | convolution fusion | flops 2421424128 | bytes 13369344 | tf_op jit(solution)/shard_map/dot_general | solution.py:986
  127.2 3.1 fusion
  130.3 2.7 multiply_reduce_fusion
  133.1 0.4 subtract_add_fusion.gh_ref
  133.5 1.7 convolution_convert_fusion.6
  135.2 1.8 convolution_convert_fusion.5
  137.0 1.8 convolution_convert_fusion.4
  138.9 1.8 convolution_convert_fusion.3
  140.7 1.8 convolution_convert_fusion.2
  142.5 4.3 %convolution_convert_fusion = bf16[3072,768]{1,0:T(8,128)(2,1)} fusion(f32[512,3072]{1,0:T(8,128)S(1)} %fusion.19, bf16[1,512,768]{2,1,0:T(8,128)(2,1)S(1)} %copy-done.3), kind=kOutput, calls=%fused_computation.3 | convolution fusion | flops 2422996992 | bytes 11796480 | tf_op jit(solution)/shard_map/dot_general | solution.py:986
  146.8 1.9 convolution_convert_fusion.1
  148.7 151.3 %attention_bwd.1 = (bf16[12,192,512]{2,1,0:T(8,128)(2,1)}, bf16[9,24,8,768]{3,2,1,0:T(8,128)(2,1)}, bf16[3,4,14,8,384]{4,3,2,1,0:T(8,128)(2,1)}) custom-call(s32[1]{0:T(128)S(6)} %copy.44.prefix_ref.refs_0_, bf16[2048,576]{1,0:T(8,128)(2,1)} %get-tuple-element.29.proj_ref.refs_1_, f32[3,3,192]{2,1,0:T(4,128)} %reshape.137.conv_ref.refs_2_, ...), custom_call_target="tpu_custom_call" | custom-call | flops 8053063680 | bytes 1572864 | tf_op jit(solution)/shard_map/attention_bwd/pallas_call | solution.py:841
  300.0 1.4 reshape.139.gone_ref
  301.4 0.7 stack.22
  302.0 0.7 stack.21
  302.7 0.8 copy.42.gains_ref
  303.5 12.7 %finish.1 = (bf16[512,768]{1,0:T(8,128)(2,1)}, f32[192,2304]{1,0:T(8,128)}, f32[192,768]{1,0:T(8,128)}, f32[192,3072]{1,0:T(8,128)}, f32[768,768]{1,0:T(8,128)}, /*index=5*/f32[8,2304]{1,0:T(8,128)}, f32[192,2]{1,0:T(8,128)}) custom-call(bf16[4,576,512]{2,1,0:T(8,128)(2,1)} %bitcast.72, bf16[216,8,768]{2,1,0:T(8,128)(2,1)} %bitcast.71, ...), custom_call_target="tpu_custom_call" | custom-call | tf_op jit(solution)/shard_map/finish/pallas_call | solution.py:962
  316.1 0.9 slice.37
  317.0 0.7 constant_dynamic-slice_fusion
  317.7 1.8 slice_reduce_fusion
  (31 shorter events, 0.6 us)
Async XLA Ops:
  76.2 39.0 %copy-start.1 = (bf16[1,512,768]{2,1,0:T(8,128)(2,1)S(1)}, bf16[1,512,768]{2,1,0:T(8,128)(2,1)}, u32[]{:S(2)}) copy-start(bf16[1,512,768]{2,1,0:T(8,128)(2,1)} %param.10) | copy-start | bytes 2359300
  76.2 39.0 %copy-start.4 = (bf16[4,1,192,768]{3,2,1,0:T(8,128)(2,1)S(1)}, bf16[4,1,192,768]{3,2,1,0:T(8,128)(2,1)}, u32[]{:S(2)}) copy-start(bf16[4,1,192,768]{3,2,1,0:T(8,128)(2,1)} %get-tuple-element.32) | copy-start | bytes 3538948
  118.8 4.9 %slice-start.2 = ((s8[4718592]{0:T(1024)(128)(4,1)}), s8[4194304]{0:T(1024)(128)(4,1)S(1)}, s32[]{:S(2)}) async-start(s8[4718592]{0:T(1024)(128)(4,1)} %bitcast.81), calls=%async_computation.2 | async-start | bytes 8388608
  119.0 4.7 %slice-start.3 = ((s8[4718592]{0:T(1024)(128)(4,1)}), s8[524288]{0:T(1024)(128)(4,1)S(1)}, s32[]{:S(2)}) async-start(s8[4718592]{0:T(1024)(128)(4,1)} %bitcast.81), calls=%async_computation.3 | async-start | bytes 1048576
  123.6 3.6 %copy-start.3 = (bf16[1,512,768]{2,1,0:T(8,128)(2,1)S(1)}, bf16[1,512,768]{2,1,0:T(8,128)(2,1)}, u32[]{:S(2)}) copy-start(bf16[1,512,768]{2,1,0:T(8,128)(2,1)} %param.19) | copy-start | bytes 2359300
  123.7 6.6 %slice-start = ((s8[4718592]{0:T(1024)(128)(4,1)}), s8[4194304]{0:T(1024)(128)(4,1)S(1)}, s32[]{:S(2)}) async-start(s8[4718592]{0:T(1024)(128)(4,1)} %bitcast.65), calls=%async_computation | async-start | bytes 8388608
  127.2 3.1 slice-start.1
  133.5 13.3 %copy-start = (f32[512,768]{1,0:T(8,128)}, f32[512,768]{1,0:T(8,128)S(1)}, u32[]{:S(2)}) copy-start(f32[512,768]{1,0:T(8,128)S(1)} %subtract_add_fusion.gh_ref) | copy-start | bytes 4718596
  142.5 4.3 %copy-start.2 = (bf16[12,64,512]{2,1,0:T(8,128)(2,1)S(1)}, bf16[12,64,512]{2,1,0:T(8,128)(2,1)}, u32[]{:S(2)}) copy-start(bf16[12,64,512]{2,1,0:T(8,128)(2,1)} %get-tuple-element.31) | copy-start | bytes 2359300

commit v3 on v2

--- a/solution.py
+++ b/solution.py
@@ -703,7 +703,7 @@
     def gp_copy(h, i, at):
         return remote(gpt.at[h, i], gp_ref.at[at * heads + h], gsend.at[h, i], grecv.at[h, at], (i, 2 * y + c, x))
 
-    ahead = min(2, sums.chunks)
+    ahead = min(0, sums.chunks)
     for k in range(ahead):
         sums.stage_b(k)
     convolve(proj_ref, conv_ref, wide, (qs, ks, vs))
@@ -866,7 +866,7 @@
 
 
 def finish_kernel(
-    gp_ref, sum_ref, own_ref, wq_ref, tok_ref, gh_ref, gone_ref, w_qkv_ref, w_up_ref, gains_ref,
+    gp_ref, sum_ref, own_ref, wq_ref, tok_ref, gh_ref, small_all, w_qkv_ref, w_up_ref, small_ref,
     gin_out, qkv_out, out_out, up_out, down_out, conv_ref, ggain_ref,
     wq, tok, gh, w_qkv, w_up, gin, qkv, out, up, down, isem, osem,
 ):
@@ -928,8 +928,11 @@
         attn = attn + jnp.sum(grad * w_qkv[:, at].astype(F32), axis=1, keepdims=True)
         conv_ref[:, at] = merge(taps, p).astype(F32)
     stores[3].start()
-    gains = gains_ref[...]
-    ggain_ref[...] = jnp.concatenate([attn / gains[:, 0:1], total / gains[:, 1:2]], axis=1)
+    columns = jnp.concatenate([jnp.broadcast_to(attn, (depth, 64)), jnp.broadcast_to(total, (depth, 64))], axis=1)
+    both = jnp.transpose(columns)
+    gains = small_ref[...].astype(F32)[0:2, :depth]
+    ggain_ref[0:1] = both[0:1] / gains[0:1]
+    ggain_ref[1:2] = both[64:65] / gains[1:2]
     for load in loads[:3]:
         load.wait()
     e1 = jnp.zeros(gh.shape, F32)
@@ -937,7 +940,8 @@
         e1 = e1 + lax.dot_general(gp_ref[j], wq[j], (((0,), (1,)), ((), ())), preferred_element_type=F32)
     x = tok[...].astype(F32)
     scale = lax.rsqrt(jnp.mean(x * x, axis=-1, keepdims=True) + 1e-06)
-    weighted = e1 * gone_ref[...]
+    gone = jnp.concatenate([small_all[s, 0, 0:1, :depth] for s in range(small_all.shape[0])], axis=1)
+    weighted = e1 * gone.astype(F32)
     back = scale * weighted - x * scale**3 * jnp.mean(weighted * x, axis=-1, keepdims=True)
     gin[...] = (gh[...] + back).astype(BF)
     stores[4].start()
@@ -945,7 +949,7 @@
         store.wait()
 
 
-def finish(gp, sums, own_sums, wq, tok, gh, gone, w_qkv, w_up, gains, ff):
+def finish(gp, sums, own_sums, wq, tok, gh, small_all, w_qkv, w_up, small, ff):
     depth, width = w_qkv.shape[0], tok.shape[1]
     vm = pl.BlockSpec(memory_space=pltpu.VMEM)
     hbm = pl.BlockSpec(memory_space=pl.ANY)
@@ -957,7 +961,7 @@
         (w_up.shape, F32),
         ((ff, width), F32),
     ]
-    flat = [((8, w_qkv.shape[1]), F32), ((depth, 2), F32)]
+    flat = [((8, w_qkv.shape[1]), F32), ((2, depth), F32)]
     kept = [(a.shape, a.dtype) for a in (wq, tok, gh, w_qkv, w_up)]
     return pl.pallas_call(
         finish_kernel,
@@ -967,7 +971,7 @@
         scratch_shapes=[pltpu.VMEM(*o) for o in kept + outs] + [dma((5,)), dma((5,))],
         compiler_params=pltpu.CompilerParams(vmem_limit_bytes=60 * 1024 * 1024),
         name="finish",
-    )(gp, sums, own_sums, wq, tok, gh, gone, w_qkv, w_up, gains)
+    )(gp, sums, own_sums, wq, tok, gh, small_all, w_qkv, w_up, small)
 
 
 def rms_scale(values):
@@ -1000,15 +1004,14 @@
     columns = w_qkv.reshape(depth, 3, blocks, heads, HEAD_DIM).transpose(2, 0, 3, 1, 4)
     gains = jnp.pad(jnp.stack([gain_attn, gain_ffn]), ((0, 0), (0, conv_w.shape[1] - depth)))
     small = jnp.pad(jnp.concatenate([gains, conv_w]), ((0, 3), (0, 0)))
-    normed_all, projected, small, full_qkv, full_out, full_up = gather_all(
+    normed_all, projected, small_all, full_qkv, full_out, full_up = gather_all(
         tokens[0], small, columns.reshape(blocks, depth, 3 * own), w_out, w_up, blocks, shards
     )
     full_qkv = full_qkv.reshape(blocks, width, 3 * own)
     full_out = full_out.reshape(width, width)
     full_up = full_up.reshape(width, -1)
-    full_gone = small[:, 0, 0, :depth].reshape(width).astype(F32)
-    full_gtwo = small[:, 0, 1, :depth].reshape(width).astype(F32)
-    full_conv = small[:, 0, 2:5].transpose(1, 0, 2)
+    full_gtwo = small_all[:, 0, 1, :depth].reshape(width).astype(F32)
+    full_conv = small_all[:, 0, 2:5].transpose(1, 0, 2)
     own_conv = lax.dynamic_index_in_dim(full_conv.reshape(3, 3, blocks, heads, HEAD_DIM), me, 2, False)
     own_conv = own_conv.transpose(2, 0, 1, 3).reshape(heads, 3, 3 * HEAD_DIM).astype(F32)
     attended_own, logsum, attended, full_down = attention_fwd(
@@ -1056,10 +1059,9 @@
     )
     grad_projected = grad_projected.reshape(blocks, 3 * own, rows)
     sums = sums.reshape(-1, 8, width)
-    gains = jnp.stack([gain_attn, gain_ffn], axis=1).astype(F32)
     grad_input, total_qkv, total_out, total_up, total_down, total_conv, grad_gains = finish(
-        grad_projected, sums, own_sums, full_qkv, tokens[0], grad_hidden, full_gone[None],
-        w_qkv, w_up, gains, w_down.shape[0],
+        grad_projected, sums, own_sums, full_qkv, tokens[0], grad_hidden, small_all,
+        w_qkv, w_up, small, w_down.shape[0],
     )
     at = lax.axis_index("shard")
     return (
@@ -1070,8 +1072,8 @@
         total_up,
         total_down,
         lax.dynamic_slice_in_dim(total_conv[:3], at * conv_w.shape[1], conv_w.shape[1], 1),
-        grad_gains[:, 0],
-        grad_gains[:, 1],
+        grad_gains[0],
+        grad_gains[1],
     )
 
 

time: 322 us -> 306 us (0.950)
  Pallas kernels: 271 us -> 262 us
  local copies, waits for them, and re-layouts: 12.8 us -> 9.01 us
    pallas_call x1, Pallas kernels: 151 us -> 143 us  [attention_bwd(): pl.pallas_call(functools.partial(bwd_kernel, counts), out_shape=(jax.Shap...]
where the time goes in v3:
time: 306 us; the launch traced here: 305 us
  Pallas kernels  262 us (86%)
  matrix products  29.6 us (10%)
  local copies, waits for them, and re-layouts  9.01 us (3%)
    pallas_call x1, Pallas kernels, attention_bwd(): pl.pallas_call(functools.partial(bwd_kernel, counts), out_shape=(jax.Shap...  143 us
    pallas_call x1, Pallas kernels, gather_all(): pl.pallas_call(gather_kernel, out_shape=[jax.ShapeDtypeStruct((width, blo...  67.7 us
    pallas_call x1, Pallas kernels, attention_fwd(): pl.pallas_call(fwd_kernel, out_shape=(jax.ShapeDtypeStruct(own, BF), jax....  39 us
    dot_general x10, matrix products, dot(): return jnp.dot(a, b, preferred_element_type=F32)  25.7 us
    pallas_call x1, Pallas kernels, finish(): pl.pallas_call(finish_kernel, out_shape=[jax.ShapeDtypeStruct(*o) for o i...  12.7 us

profile of v3, /device:TPU:0, one launch (start us, length us, event | category | flops | bytes accessed | tf_op | source)
XLA Modules:
  0.0 305.2 jit_solution(6173777009356373295)
XLA Ops:
  1.3 0.7 stack.9
  2.0 0.7 stack.10
  2.6 1.3 fusion.12
  3.9 1.5 copy.21
  5.5 0.1 copy.22
  5.6 1.3 copy.23.qkv_ref
  6.9 67.7 %gather_all.1 = (bf16[768,2048]{1,0:T(8,128)(2,1)}, bf16[2048,576]{1,0:T(8,128)(2,1)}, bf16[4,1,8,576]{3,2,1,0:T(8,128)(2,1)}, bf16[4,4,192,576]{3,2,1,0:T(8,128...) custom-call(bf16[512,768]{1,0:T(8,128)(2,1)} %bitcast.69, ...), custom_call_target="tpu_custom_call" | custom-call | tf_op jit(solution)/shard_map/gather_all/pallas_call | solution.py:283
  74.6 0.7 convert_reduce_fusion
  75.4 0.8 slice_bitcast_fusion
  76.3 0.1 reshape.109
  76.4 0.7 reshape.125.conv_ref.refs_2_
  77.1 39.0 %attention_fwd.1 = (bf16[3,4,64,512]{3,2,1,0:T(8,128)(2,1)}, f32[3,8,2048]{2,1,0:T(8,128)}, bf16[12,64,512]{2,1,0:T(8,128)(2,1)}, bf16[4,4,192,768]{3,2,1,0:T(8,128)(2,1)}) custom-call(s32[1]{0:T(128)S(6)} %copy.28.prefix_ref.refs_0_, bf16[2048,576]{1,0:T(8,128)(2,1)} %get-tuple-element.29.proj_ref.refs_1_, f32[3,3,192]{2,1,0:T(4,128)} %reshape.125.conv_ref.refs_2_, ...), custom_call_target="tpu_custom_call" | custom-call | flops 3221225472 | bytes 2359296 | tf_op jit(solution)/shard_map/attention_fwd/pallas_call | solution.py:380
  116.1 2.2 multiply_reduce_fusion.1
  118.3 0.2 multiply_convert_fusion.1
  118.5 0.1 copy-done.1
  118.7 2.6 fusion.20
  121.3 3.6 %fusion.1 = bf16[1,512,768]{2,1,0:T(8,128)(2,1)} fusion(f32[512,768]{1,0:T(8,128)S(1)} %get-tuple-element.56, bf16[3072,768]{1,0:T(8,128)(2,1)S(1)} %bitcast.86, f32[512,3072]{1,0:T(8,128)S(1)} %fusion.20), kind=kOutput, calls=%fused_computation.17 | convolution fusion | flops 2421424128 | bytes 13369344 | tf_op jit(solution)/shard_map/dot_general | solution.py:990
  124.9 2.9 fusion
  127.8 2.8 multiply_reduce_fusion
  130.6 4.5 %convolution_convert_fusion = bf16[3072,768]{1,0:T(8,128)(2,1)} fusion(f32[512,3072]{1,0:T(8,128)S(1)} %fusion.20, bf16[1,512,768]{2,1,0:T(8,128)(2,1)S(1)} %copy-done.4), kind=kOutput, calls=%fused_computation.3 | convolution fusion | flops 2422996992 | bytes 11796480 | tf_op jit(solution)/shard_map/dot_general | solution.py:990
  135.1 0.4 subtract_add_fusion.gh_ref
  135.6 1.7 convolution_convert_fusion.6
  137.3 1.9 convolution_convert_fusion.1
  139.2 1.9 convolution_convert_fusion.2
  141.0 1.8 convolution_convert_fusion.3
  142.9 1.8 convolution_convert_fusion.4
  144.7 1.8 convolution_convert_fusion.5
  146.5 143.0 %attention_bwd.1 = (bf16[12,192,512]{2,1,0:T(8,128)(2,1)}, bf16[9,24,8,768]{3,2,1,0:T(8,128)(2,1)}, bf16[3,4,14,8,384]{4,3,2,1,0:T(8,128)(2,1)}) custom-call(s32[1]{0:T(128)S(6)} %copy.28.prefix_ref.refs_0_, bf16[2048,576]{1,0:T(8,128)(2,1)} %get-tuple-element.29.proj_ref.refs_1_, f32[3,3,192]{2,1,0:T(4,128)} %reshape.125.conv_ref.refs_2_, ...), custom_call_target="tpu_custom_call" | custom-call | flops 8053063680 | bytes 1572864 | tf_op jit(solution)/shard_map/attention_bwd/pallas_call | solution.py:841
  289.5 12.7 %finish.1 = (bf16[512,768]{1,0:T(8,128)(2,1)}, f32[192,2304]{1,0:T(8,128)}, f32[192,768]{1,0:T(8,128)}, f32[192,3072]{1,0:T(8,128)}, f32[768,768]{1,0:T(8,128)}, /*index=5*/f32[8,2304]{1,0:T(8,128)}, f32[2,192]{1,0:T(2,128)}) custom-call(bf16[4,576,512]{2,1,0:T(8,128)(2,1)} %bitcast.72, bf16[216,8,768]{2,1,0:T(8,128)(2,1)} %bitcast.71, ...), custom_call_target="tpu_custom_call" | custom-call | tf_op jit(solution)/shard_map/finish/pallas_call | solution.py:966
  302.3 1.3 fusion.19
  303.6 0.9 slice.33
  304.5 0.7 constant_dynamic-slice_fusion
  (23 shorter events, 0.2 us)
Async XLA Ops:
  77.1 39.0 %copy-start.2 = (bf16[1,512,768]{2,1,0:T(8,128)(2,1)S(1)}, bf16[1,512,768]{2,1,0:T(8,128)(2,1)}, u32[]{:S(2)}) copy-start(bf16[1,512,768]{2,1,0:T(8,128)(2,1)} %param.10) | copy-start | bytes 2359300
  77.1 39.0 %copy-start.5 = (bf16[4,1,192,768]{3,2,1,0:T(8,128)(2,1)S(1)}, bf16[4,1,192,768]{3,2,1,0:T(8,128)(2,1)}, u32[]{:S(2)}) copy-start(bf16[4,1,192,768]{3,2,1,0:T(8,128)(2,1)} %get-tuple-element.32) | copy-start | bytes 3538948
  116.1 2.6 copy-start.1
  118.3 3.0 slice-start
  118.7 2.6 slice-start.1
  121.3 3.6 %copy-start.4 = (bf16[1,512,768]{2,1,0:T(8,128)(2,1)S(1)}, bf16[1,512,768]{2,1,0:T(8,128)(2,1)}, u32[]{:S(2)}) copy-start(bf16[1,512,768]{2,1,0:T(8,128)(2,1)} %param.19) | copy-start | bytes 2359300
  135.5 3.6 %copy-start = (f32[512,768]{1,0:T(8,128)}, f32[512,768]{1,0:T(8,128)S(1)}, u32[]{:S(2)}) copy-start(f32[512,768]{1,0:T(8,128)S(1)} %subtract_add_fusion.gh_ref) | copy-start | bytes 4718596
  135.5 1.7 copy-start.3

commit v4 on v3

--- a/solution.py
+++ b/solution.py
@@ -690,7 +690,6 @@
     own = OwnSums(sums, own_part, own_ref, own_bufs, own_sems)
     z, y, c, x = sums.me
     greet(sums.peers())
-    sums.start()
 
     def block_copy(h, i, at):
         return remote(do_ref.at[i * heads + h], dos.at[h, at], send.at[h, i], recv.at[h, at], (i, 2 * y + c, x))
@@ -699,6 +698,7 @@
         for i in range(1, blocks):
             block_copy(h, (z + i) % blocks, z).start()
         dos[h, z] = do_ref[z * heads + h]
+    sums.start()
 
     def gp_copy(h, i, at):
         return remote(gpt.at[h, i], gp_ref.at[at * heads + h], gsend.at[h, i], grecv.at[h, at], (i, 2 * y + c, x))
@@ -798,6 +798,8 @@
     for n, stage in enumerate(own.stages()):
         sums.step(turns + n)
         stage(heads - 1)
+    for n in range(1, blocks):
+        gp_copy(heads - 1, (z + n) % blocks, z).start()
     def forward(h, _):
         own.stage_f(h)
         return 0
@@ -809,8 +811,6 @@
         sums.step(t)
         return 0
     lax.fori_loop(turns + count, max(sums.chunks + sums.LAGS[-1], turns + count), tail, 0)
-    for n in range(1, blocks):
-        gp_copy(heads - 1, (z + n) % blocks, z).start()
     sums.finish()
     def done(h, _):
         own.finish(h)

time: 306 us -> 306 us (level)
  no operation moved by 1% of the time
where the time goes in v4:
time: 306 us; the launch traced here: 305 us
  Pallas kernels  262 us (86%)
  matrix products  29.6 us (10%)
  local copies, waits for them, and re-layouts  9.01 us (3%)
    pallas_call x1, Pallas kernels, attention_bwd(): pl.pallas_call(functools.partial(bwd_kernel, counts), out_shape=(jax.Shap...  143 us
    pallas_call x1, Pallas kernels, gather_all(): pl.pallas_call(gather_kernel, out_shape=[jax.ShapeDtypeStruct((width, blo...  67.7 us
    pallas_call x1, Pallas kernels, attention_fwd(): pl.pallas_call(fwd_kernel, out_shape=(jax.ShapeDtypeStruct(own, BF), jax....  39 us
    dot_general x10, matrix products, dot(): return jnp.dot(a, b, preferred_element_type=F32)  25.7 us
    pallas_call x1, Pallas kernels, finish(): pl.pallas_call(finish_kernel, out_shape=[jax.ShapeDtypeStruct(*o) for o i...  12.7 us

profile of v4, /device:TPU:0, one launch (start us, length us, event | category | flops | bytes accessed | tf_op | source)
XLA Modules:
  0.0 305.1 jit_solution(1987757996411424794)
XLA Ops:
  1.3 0.7 stack.9
  2.0 0.7 stack.10
  2.6 1.3 fusion.12
  3.9 1.5 copy.21
  5.5 0.1 copy.22
  5.6 1.3 copy.23.qkv_ref
  6.9 67.7 %gather_all.1 = (bf16[768,2048]{1,0:T(8,128)(2,1)}, bf16[2048,576]{1,0:T(8,128)(2,1)}, bf16[4,1,8,576]{3,2,1,0:T(8,128)(2,1)}, bf16[4,4,192,576]{3,2,1,0:T(8,128...) custom-call(bf16[512,768]{1,0:T(8,128)(2,1)} %bitcast.69, ...), custom_call_target="tpu_custom_call" | custom-call | tf_op jit(solution)/shard_map/gather_all/pallas_call | solution.py:283
  74.6 0.7 convert_reduce_fusion
  75.4 0.8 slice_bitcast_fusion
  76.3 0.1 reshape.109
  76.4 0.7 reshape.125.conv_ref.refs_2_
  77.1 39.0 %attention_fwd.1 = (bf16[3,4,64,512]{3,2,1,0:T(8,128)(2,1)}, f32[3,8,2048]{2,1,0:T(8,128)}, bf16[12,64,512]{2,1,0:T(8,128)(2,1)}, bf16[4,4,192,768]{3,2,1,0:T(8,128)(2,1)}) custom-call(s32[1]{0:T(128)S(6)} %copy.28.prefix_ref.refs_0_, bf16[2048,576]{1,0:T(8,128)(2,1)} %get-tuple-element.29.proj_ref.refs_1_, f32[3,3,192]{2,1,0:T(4,128)} %reshape.125.conv_ref.refs_2_, ...), custom_call_target="tpu_custom_call" | custom-call | flops 3221225472 | bytes 2359296 | tf_op jit(solution)/shard_map/attention_fwd/pallas_call | solution.py:380
  116.1 2.2 multiply_reduce_fusion.1
  118.3 0.2 multiply_convert_fusion.1
  118.5 0.1 copy-done.1
  118.7 2.6 fusion.20
  121.3 3.6 %fusion.1 = bf16[1,512,768]{2,1,0:T(8,128)(2,1)} fusion(f32[512,768]{1,0:T(8,128)S(1)} %get-tuple-element.56, bf16[3072,768]{1,0:T(8,128)(2,1)S(1)} %bitcast.86, f32[512,3072]{1,0:T(8,128)S(1)} %fusion.20), kind=kOutput, calls=%fused_computation.17 | convolution fusion | flops 2421424128 | bytes 13369344 | tf_op jit(solution)/shard_map/dot_general | solution.py:990
  124.9 2.9 fusion
  127.8 2.8 multiply_reduce_fusion
  130.6 4.5 %convolution_convert_fusion = bf16[3072,768]{1,0:T(8,128)(2,1)} fusion(f32[512,3072]{1,0:T(8,128)S(1)} %fusion.20, bf16[1,512,768]{2,1,0:T(8,128)(2,1)S(1)} %copy-done.4), kind=kOutput, calls=%fused_computation.3 | convolution fusion | flops 2422996992 | bytes 11796480 | tf_op jit(solution)/shard_map/dot_general | solution.py:990
  135.1 0.4 subtract_add_fusion.gh_ref
  135.6 1.7 convolution_convert_fusion.6
  137.3 1.9 convolution_convert_fusion.1
  139.2 1.9 convolution_convert_fusion.2
  141.0 1.8 convolution_convert_fusion.3
  142.9 1.8 convolution_convert_fusion.4
  144.7 1.8 convolution_convert_fusion.5
  146.5 142.9 %attention_bwd.1 = (bf16[12,192,512]{2,1,0:T(8,128)(2,1)}, bf16[9,24,8,768]{3,2,1,0:T(8,128)(2,1)}, bf16[3,4,14,8,384]{4,3,2,1,0:T(8,128)(2,1)}) custom-call(s32[1]{0:T(128)S(6)} %copy.28.prefix_ref.refs_0_, bf16[2048,576]{1,0:T(8,128)(2,1)} %get-tuple-element.29.proj_ref.refs_1_, f32[3,3,192]{2,1,0:T(4,128)} %reshape.125.conv_ref.refs_2_, ...), custom_call_target="tpu_custom_call" | custom-call | flops 8053063680 | bytes 1572864 | tf_op jit(solution)/shard_map/attention_bwd/pallas_call | solution.py:841
  289.4 12.7 %finish.1 = (bf16[512,768]{1,0:T(8,128)(2,1)}, f32[192,2304]{1,0:T(8,128)}, f32[192,768]{1,0:T(8,128)}, f32[192,3072]{1,0:T(8,128)}, f32[768,768]{1,0:T(8,128)}, /*index=5*/f32[8,2304]{1,0:T(8,128)}, f32[2,192]{1,0:T(2,128)}) custom-call(bf16[4,576,512]{2,1,0:T(8,128)(2,1)} %bitcast.72, bf16[216,8,768]{2,1,0:T(8,128)(2,1)} %bitcast.71, ...), custom_call_target="tpu_custom_call" | custom-call | tf_op jit(solution)/shard_map/finish/pallas_call | solution.py:966
  302.2 1.3 fusion.19
  303.5 0.9 slice.33
  304.4 0.7 constant_dynamic-slice_fusion
  (23 shorter events, 0.2 us)
Async XLA Ops:
  77.1 39.0 %copy-start.2 = (bf16[1,512,768]{2,1,0:T(8,128)(2,1)S(1)}, bf16[1,512,768]{2,1,0:T(8,128)(2,1)}, u32[]{:S(2)}) copy-start(bf16[1,512,768]{2,1,0:T(8,128)(2,1)} %param.10) | copy-start | bytes 2359300
  77.1 39.0 %copy-start.5 = (bf16[4,1,192,768]{3,2,1,0:T(8,128)(2,1)S(1)}, bf16[4,1,192,768]{3,2,1,0:T(8,128)(2,1)}, u32[]{:S(2)}) copy-start(bf16[4,1,192,768]{3,2,1,0:T(8,128)(2,1)} %get-tuple-element.32) | copy-start | bytes 3538948
  116.1 2.6 copy-start.1
  118.3 3.0 slice-start
  118.7 2.6 slice-start.1
  121.3 3.6 %copy-start.4 = (bf16[1,512,768]{2,1,0:T(8,128)(2,1)S(1)}, bf16[1,512,768]{2,1,0:T(8,128)(2,1)}, u32[]{:S(2)}) copy-start(bf16[1,512,768]{2,1,0:T(8,128)(2,1)} %param.19) | copy-start | bytes 2359300
  135.5 3.6 %copy-start = (f32[512,768]{1,0:T(8,128)}, f32[512,768]{1,0:T(8,128)S(1)}, u32[]{:S(2)}) copy-start(f32[512,768]{1,0:T(8,128)S(1)} %subtract_add_fusion.gh_ref) | copy-start | bytes 4718596
  135.5 1.7 copy-start.3
